TPU v7x, 32 devices: a whole 2x2x4 slice. The times are simulated.
32 devices in a mesh: ha: 8 (over z, x), ta: 4 (over y, core).
Axes of the slice: x: 2, y: 2, z: 4, core: 2. Of those that a mesh axis runs over, the one named last changes fastest.
Arguments:
- layer_input: bfloat16 [8, 24, 192, 128], P('ta', 'ha'), may hold values from -6 to 6
- pre_one: bfloat16 [8, 24, 192, 128], P('ta', 'ha'), may hold values from -9 to 9
- pre_two: bfloat16 [8, 24, 192, 128], P('ta', 'ha'), may hold values from -9 to 9
- pre_three: bfloat16 [8, 24, 192, 128], P('ta', 'ha'), may hold values from -9 to 9
- kernel_one: bfloat16 [3, 3, 3, 128, 128], replicated, may hold values from -0.109375 to 0.109375
- kernel_two: bfloat16 [3, 3, 3, 128, 128], replicated, may hold values from -0.109375 to 0.109375
- kernel_three: bfloat16 [3, 3, 3, 128, 128], replicated, may hold values from -0.109375 to 0.109375
- upstream: bfloat16 [8, 24, 192, 128], P('ta', 'ha'), may hold values from -24 to 24
Outputs:
- input_gradient: bfloat16 [8, 24, 192, 128], P('ta', 'ha')
- kernel_grad_one: float32 [3, 3, 3, 128, 128], P(None, None, None, 'ha')
- kernel_grad_two: float32 [3, 3, 3, 128, 128], P(None, None, None, 'ha')
- kernel_grad_three: float32 [3, 3, 3, 128, 128], P(None, None, None, 'ha')
All inputs are finite; a program needn't handle non-finite values.
Results may differ from a plain program's by a relative error of at most 0.014.
Values may be sent and summed in bfloat16 or wider, within the bound.
A program may use at most 128 MiB of HBM per device.

v0:
```python
import math

import jax
import jax.numpy as jnp
from jax import lax
from jax.sharding import PartitionSpec as P


def from_behind(block, axis, distance):
    devices = range(lax.axis_size(axis))
    route = [(i - distance, i) for i in devices if i - distance in devices]
    return lax.ppermute(block, axis, route)


def padded(x, sides, width):
    for axis, dim in sides:
        peers, length = (lax.axis_size(axis), x.shape[dim])
        up = [(i, (i + 1) % peers) for i in range(peers - 1)]
        down = [(j, i) for i, j in up]
        last = lax.slice_in_dim(x, length - width, length, axis=dim)
        initial = lax.slice_in_dim(x, 0, width, axis=dim)
        before = lax.ppermute(last, axis, up)
        after = lax.ppermute(initial, axis, down)
        x = jnp.concatenate([before, x, after], axis=dim)
    return x


def silu_slope(pre_values):
    values = pre_values.astype(jnp.float32)
    sigmoid = jax.nn.sigmoid(values)
    return sigmoid * (1.0 + values * (1.0 - sigmoid))


def forward_taps(widened, frame_count, row_count, col_count):
    tap_list = [
        widened[
            tap_time : tap_time + frame_count,
            tap_row : tap_row + row_count,
            tap_col : tap_col + col_count,
        ]
        for tap_time in range(3)
        for tap_row in range(3)
        for tap_col in range(3)
    ]
    patches = jnp.concatenate(tap_list, -1)
    return patches.reshape(-1, patches.shape[-1])


def gather_grad(gradient, kernel):
    frame_count, row_count, col_count, channels = gradient.shape
    ahead = from_behind(gradient, "ta", -1)
    joined = jnp.concatenate([gradient, ahead], 0)
    rimmed = padded(joined, (("ha", 1),), 1)
    widened = jnp.pad(rimmed, ((0, 0), (0, 0), (1, 1), (0, 0)))
    tap_list = [
        widened[
            2 - tap_time : 2 - tap_time + frame_count,
            2 - tap_row : 2 - tap_row + row_count,
            2 - tap_col : 2 - tap_col + col_count,
        ]
        for tap_time in range(3)
        for tap_row in range(3)
        for tap_col in range(3)
    ]
    patches = jnp.concatenate(tap_list, -1).reshape(-1, 27 * channels)
    flipped = jnp.swapaxes(kernel, 3, 4).reshape(27 * channels, channels)
    result = jnp.dot(patches, flipped, preferred_element_type=jnp.float32)
    return result.reshape(frame_count, row_count, col_count, channels)


def input_grad(gradient, kernel):
    return gather_grad(gradient, kernel)


def own_block(full_term, channels, piece_width):
    shaped = full_term.reshape(3, 3, 3, channels, channels)
    return lax.dynamic_slice_in_dim(shaped, lax.axis_index("ha") * piece_width, piece_width, 3)


def shards(
    layer_input, pre_one, pre_two, pre_three, kernel_one, kernel_two, kernel_three, upstream
):
    frame_count, row_count, col_count, channels = layer_input.shape
    piece_width = channels // lax.axis_size("ha")
    cells_total = frame_count * row_count * col_count * lax.axis_size("ta") * lax.axis_size("ha")
    norm_scale = 1.0 / math.sqrt(cells_total)
    act_one = jax.nn.silu(pre_one.astype(jnp.float32)).astype(jnp.bfloat16)
    act_two = jax.nn.silu(pre_two.astype(jnp.float32)).astype(jnp.bfloat16)
    stacked = jnp.stack([layer_input, act_one, act_two], 0)
    earlier = from_behind(stacked, "ta", 1)
    joined = jnp.concatenate([earlier, stacked], 1)
    rimmed = padded(joined, (("ha", 2),), 1)
    widened = jnp.pad(rimmed, ((0, 0), (0, 0), (0, 0), (1, 1), (0, 0)))
    gradient = (upstream.astype(jnp.float32) * silu_slope(pre_three)).astype(jnp.bfloat16)
    layer_list = [(kernel_three, pre_two, 2), (kernel_two, pre_one, 1), (kernel_one, None, 0)]
    reduced = []
    input_gradient = None
    for kernel, previous, depth_index in layer_list:
        patches = forward_taps(widened[depth_index], frame_count, row_count, col_count)
        grad_flat = gradient.reshape(-1, channels)
        local_term = lax.dot_general(
            patches, grad_flat, (((0,), (0,)), ((), ())), preferred_element_type=jnp.float32
        )
        summed_one = lax.psum(local_term, ("ha", "ta"))
        reduced.append(own_block(summed_one, channels, piece_width) * norm_scale)
        back_grad = input_grad(gradient, kernel)
        if previous is None:
            input_gradient = back_grad.astype(jnp.bfloat16)
        else:
            gradient = (back_grad * silu_slope(previous)).astype(jnp.bfloat16)
    return (input_gradient, reduced[2], reduced[1], reduced[0])


def solution(mesh):
    return jax.shard_map(
        shards,
        mesh=mesh,
        in_specs=(
            P("ta", "ha", None, None),
            P("ta", "ha", None, None),
            P("ta", "ha", None, None),
            P("ta", "ha", None, None),
            P(),
            P(),
            P(),
            P("ta", "ha", None, None),
        ),
        out_specs=(
            P("ta", "ha", None, None),
            P(None, None, None, "ha", None),
            P(None, None, None, "ha", None),
            P(None, None, None, "ha", None),
        ),
        check_vma=False,
    )
```

profile of v0, /device:TPU:0, one launch (start us, length us, event | category | flops | bytes accessed | tf_op | source)
XLA Modules:
  0.0 287.2 jit_solution(15217479675457381157)
XLA Ops:
  7.2 1.3 fusion.34
  8.5 1.3 collective-permute-start
  9.8 1.1 fusion.47
  10.9 1.0 collective-permute-done
  12.0 4.9 %collective-permute-start.1 = (bf16[4,1,192,128]{3,2,1,0:T(8,128)(2,1)S(1)}, bf16[4,1,192,128]{3,2,1,0:T(8,128)(2,1)S(1)}, u32[]{:S(2)}, u32[]{:S(2)}) collective-permute-start(bf16[4,1,192,128]{3,2,1,0:T(8,128)(2,1)S(1)} %get-tuple-element.22), channel_id=1, source_target_pairs={{0,4},{4,8},{8,12},{12,16},{16,20},{20,24},{24,28},{1,5},{5,9},{9,... | collective-permute-start | bytes 589832 | tf_op jit(solution)/shard_map/ppermute | solution.py:22
  16.9 1.3 collective-permute-start.2
  18.2 1.1 fusion.48
  19.3 2.0 pad_maximum_fusion
  21.4 6.1 %collective-permute-start.9 = (bf16[3,2,3,192,128]{4,3,2,1,0:T(8,128)(2,1)}, bf16[3,2,3,192,128]{4,3,2,1,0:T(8,128)(2,1)S(1)}, u32[]{:S(2)}, u32[]{:S(2)}) collective-permute-start(bf16[3,2,3,192,128]{4,3,2,1,0:T(8,128)(2,1)} %pad_maximum_fusion), channel_id=1, source_target_pairs={{0,1},{1,2},{2,3},{4,5},{5,6},{6,7},{8,9},{9,10},{10,11},{12,13},{... | collective-permute-start | bytes 2654216 | tf_op jit(solution)/shard_map/ppermute | solution.py:12
  27.5 2.3 copy.12
  32.8 2.3 fusion.9
  35.1 1.3 collective-permute-start.3
  36.4 2.2 collective-permute-done.3
  38.6 4.3 %collective-permute-start.4 = (bf16[4,1,192,128]{3,2,1,0:T(8,128)(2,1)S(1)}, bf16[4,1,192,128]{3,2,1,0:T(8,128)(2,1)S(1)}, u32[]{:S(2)}, u32[]{:S(2)}) collective-permute-start(bf16[4,1,192,128]{3,2,1,0:T(8,128)(2,1)S(1)} %get-tuple-element.18), channel_id=1, source_target_pairs={{0,4},{4,8},{8,12},{12,16},{16,20},{20,24},{24,28},{1,5},{5,9},{9,... | collective-permute-start | bytes 589832 | tf_op jit(solution)/shard_map/ppermute | solution.py:22
  42.9 1.3 collective-permute-start.5
  44.2 2.3 copy.13
  46.5 1.2 pad_maximum_fusion.7
  47.7 5.8 %collective-permute-start.10 = (bf16[3,4,1,192,128]{4,3,2,1,0:T(8,128)(2,1)}, bf16[3,4,1,192,128]{4,3,2,1,0:T(8,128)(2,1)}, u32[]{:S(2)}, u32[]{:S(2)}) collective-permute-start(bf16[3,4,1,192,128]{4,3,2,1,0:T(8,128)(2,1)} %get-tuple-element.10), channel_id=1, source_target_pairs={{0,4},{4,8},{8,12},{12,16},{16,20},{20,24},{24,28},{1,5},{5,9},{9,... | collective-permute-start | bytes 1769480 | tf_op jit(solution)/shard_map/ppermute | solution.py:22
  53.4 1.3 collective-permute-start.11
  57.8 2.3 fusion.10
  60.1 1.3 collective-permute-start.6
  61.4 2.3 copy.14
  63.7 3.7 %collective-permute-done.6 = bf16[2,3,192,128]{3,2,1,0:T(8,128)(2,1)S(1)} collective-permute-done((bf16[2,3,192,128]{3,2,1,0:T(8,128)(2,1)S(1)}, bf16[2,3,192,128]{3,2,1,0:T(8,128)(2,1)S(1)}, u32[]{:S(2)}, u32[]{:S(2)}) %collective-permute-start.6) | collective-permute-done | bytes 294944 | tf_op jit(solution)/shard_map/ppermute | solution.py:12
  67.4 4.4 %collective-permute-start.7 = (bf16[4,1,192,128]{3,2,1,0:T(8,128)(2,1)S(1)}, bf16[4,1,192,128]{3,2,1,0:T(8,128)(2,1)S(1)}, u32[]{:S(2)}, u32[]{:S(2)}) collective-permute-start(bf16[4,1,192,128]{3,2,1,0:T(8,128)(2,1)S(1)} %get-tuple-element.14), channel_id=1, source_target_pairs={{0,4},{4,8},{8,12},{12,16},{16,20},{20,24},{24,28},{1,5},{5,9},{9,... | collective-permute-start | bytes 589832 | tf_op jit(solution)/shard_map/ppermute | solution.py:22
  71.8 1.3 collective-permute-start.8
  73.1 4.7 %collective-permute-done.10 = bf16[3,4,1,192,128]{4,3,2,1,0:T(8,128)(2,1)} collective-permute-done((bf16[3,4,1,192,128]{4,3,2,1,0:T(8,128)(2,1)}, bf16[3,4,1,192,128]{4,3,2,1,0:T(8,128)(2,1)}, u32[]{:S(2)}, u32[]{:S(2)}) %collective-permute-start.10) | collective-permute-done | bytes 589856 | tf_op jit(solution)/shard_map/ppermute | solution.py:22
  77.8 3.9 %select_maximum_fusion = bf16[3,4,5,194,128]{4,3,2,1,0:T(8,128)(2,1)S(1)} fusion(bf16[3,4,1,192,128]{4,3,2,1,0:T(8,128)(2,1)} %collective-permute-done.11, bf16[3,4,1,192,128]{4,3,2,1,0:T(8,128)(2,1)} %collective-permute-done.10, bf16[3,2,3,192,128]{4,3,2,1,0:T(8,128)(2,1)S(1)} %collective-permute-done.9, bf16[1,2,3,192,128]{4,3,2,1,0:T(8,128)(2,1)S(1)} %fusion.48, ...), kind=kLoop, calls=%fused_computation.5 | loop fusion | flops 31288320 | bytes 5928960 | tf_op jit(solution)/shard_map/concatenate | solution.py:24
  88.0 3.6 %fusion.56 = f32[3456,128,1,1]{1,0,3,2:T(8,128)} fusion(bf16[2,3,192,3456]{3,2,1,0:T(8,128)(2,1)S(1)} %get-tuple-element.25, bf16[2,3,192,128]{3,2,1,0:T(8,128)(2,1)S(1)} %fusion.9), kind=kOutput, calls=%fused_computation.269 | convolution fusion | flops 1019215872 | bytes 10027008 | tf_op jit(solution)/shard_map/dot_general | solution.py:101
  91.6 3.6 %fusion.55 = f32[3456,128,1,1]{1,0,3,2:T(8,128)} fusion(bf16[2,3,192,3456]{3,2,1,0:T(8,128)(2,1)S(1)} %get-tuple-element.24, bf16[2,3,192,128]{3,2,1,0:T(8,128)(2,1)S(1)} %fusion.10), kind=kOutput, calls=%fused_computation.268 | convolution fusion | flops 1019215872 | bytes 10027008 | tf_op jit(solution)/shard_map/dot_general | solution.py:101
  98.5 3.7 %fusion.57 = f32[3456,128,1,1]{1,0,3,2:T(8,128)} fusion(bf16[2,3,192,3456]{3,2,1,0:T(8,128)(2,1)S(1)} %constant_dynamic-update-slice_fusion.135, bf16[2,3,192,128]{3,2,1,0:T(8,128)(2,1)S(1)} %fusion.34), kind=kOutput, calls=%fused_computation.270 | convolution fusion | flops 1019215872 | bytes 10027008 | tf_op jit(solution)/shard_map/dot_general | solution.py:101
  102.4 0.8 constant_dynamic-update-slice_fusion.80
  104.1 0.8 constant_dynamic-update-slice_fusion.78
  104.9 0.8 constant_dynamic-update-slice_fusion.77
  107.3 0.9 constant_dynamic-update-slice_fusion.74
  108.2 0.8 constant_dynamic-update-slice_fusion.73
  109.0 0.8 constant_dynamic-update-slice_fusion.72
  109.8 0.8 constant_dynamic-update-slice_fusion.71
  110.6 0.8 constant_dynamic-update-slice_fusion.70
  112.1 0.9 constant_dynamic-update-slice_fusion.68
  114.6 0.8 constant_dynamic-update-slice_fusion.65
  117.0 0.8 constant_dynamic-update-slice_fusion.62
  119.3 0.8 constant_dynamic-update-slice_fusion.59
  121.7 0.8 constant_dynamic-update-slice_fusion.56
  124.1 6.4 %convolution_convert_fusion = bf16[2,3,192,128]{3,2,1,0:T(8,128)(2,1)} fusion(bf16[2,3,192,3456]{3,2,1,0:T(8,128)(2,1)} %constant_dynamic-update-slice_fusion.54, bf16[3456,128,1,1]{1,0,3,2:T(8,128)(2,1)} %bitcast.65), kind=kOutput, calls=%fused_computation.19 | convolution fusion | flops 1019363328 | bytes 9142272 | tf_op jit(solution)/shard_map/dot_general | solution.py:67
  130.4 145.0 %all-reduce.7.cloned.1.call-done = (f32[3,3,3,128,128]{4,3,2,1,0:T(8,128)}, f32[3,3,3,128,128]{4,3,2,1,0:T(8,128)}, f32[3,3,3,128,128]{4,3,2,1,0:T(8,128)}) async-done(((f32[3,3,3,128,128]{4,3,2,1,0:T(8,128)}, f32[3,3,3,128,128]{4,3,2,1,0:T(8,128)}, f32[3,3,3,128,128]{4,3,2,1,0:T(8,128)}), (f32[3,3,3,128,128]{4,3,2,1,0:T(8,128)}, f32[3,3,3,128,128]{4,3,2,1,0:T(8,128)}, ...) | async-done | bytes 5308432 | tf_op jit(solution)/shard_map/psum | solution.py:104
  275.4 1.6 dynamic-slice_multiply_fusion
  277.1 1.6 dynamic-slice_multiply_fusion.1
  278.7 1.6 dynamic-slice_multiply_fusion.2
  (178 shorter events, 25.8 us)
Async XLA Ops:
  7.2 268.3 %all-reduce.7.cloned.1.call-start = ((), (), s32[]{:S(2)}) async-start(), calls=%async_computation | async-start | bytes 10616832 | tf_op jit(solution)/shard_map/psum | solution.py:104
  8.5 3.5 %collective-permute-start = (bf16[2,3,192,128]{3,2,1,0:T(8,128)(2,1)S(1)}, bf16[2,3,192,128]{3,2,1,0:T(8,128)(2,1)S(1)}, u32[]{:S(2)}, u32[]{:S(2)}) collective-permute-start(bf16[2,3,192,128]{3,2,1,0:T(8,128)(2,1)S(1)} %fusion.34), channel_id=1, source_target_pairs={{1,0},{2,1},{3,2},{5,4},{6,5},{7,6},{9,8},{10,9},{11,10},{13,12},{... | collective-permute-start | bytes 884744 | tf_op jit(solution)/shard_map/ppermute | solution.py:12
  12.0 17.8 %collective-permute-start.1 = (bf16[4,1,192,128]{3,2,1,0:T(8,128)(2,1)S(1)}, bf16[4,1,192,128]{3,2,1,0:T(8,128)(2,1)S(1)}, u32[]{:S(2)}, u32[]{:S(2)}) collective-permute-start(bf16[4,1,192,128]{3,2,1,0:T(8,128)(2,1)S(1)} %get-tuple-element.22), channel_id=1, source_target_pairs={{0,4},{4,8},{8,12},{12,16},{16,20},{20,24},{24,28},{1,5},{5,9},{9,... | collective-permute-start | bytes 589832 | tf_op jit(solution)/shard_map/ppermute | solution.py:22
  16.9 12.9 %collective-permute-start.2 = (bf16[4,1,192,128]{3,2,1,0:T(8,128)(2,1)S(1)}, bf16[4,1,192,128]{3,2,1,0:T(8,128)(2,1)S(1)}, u32[]{:S(2)}, u32[]{:S(2)}) collective-permute-start(bf16[4,1,192,128]{3,2,1,0:T(8,128)(2,1)S(1)} %get-tuple-element.23), channel_id=1, source_target_pairs={{4,0},{8,4},{12,8},{16,12},{20,16},{24,20},{28,24},{5,1},{9,5},{13... | collective-permute-start | bytes 589832 | tf_op jit(solution)/shard_map/ppermute | solution.py:23
  21.4 25.1 %collective-permute-start.9 = (bf16[3,2,3,192,128]{4,3,2,1,0:T(8,128)(2,1)}, bf16[3,2,3,192,128]{4,3,2,1,0:T(8,128)(2,1)S(1)}, u32[]{:S(2)}, u32[]{:S(2)}) collective-permute-start(bf16[3,2,3,192,128]{4,3,2,1,0:T(8,128)(2,1)} %pad_maximum_fusion), channel_id=1, source_target_pairs={{0,1},{1,2},{2,3},{4,5},{5,6},{6,7},{8,9},{9,10},{10,11},{12,13},{... | collective-permute-start | bytes 2654216 | tf_op jit(solution)/shard_map/ppermute | solution.py:12
  30.3 2.5 copy-start.2
  30.3 2.5 copy-start.3
  32.8 13.7 %copy-start = (bf16[2,3,192,128]{3,2,1,0:T(8,128)(2,1)S(1)}, bf16[2,3,192,128]{3,2,1,0:T(8,128)(2,1)}, u32[]{:S(2)}) copy-start(bf16[2,3,192,128]{3,2,1,0:T(8,128)(2,1)} %param.8) | copy-start | bytes 884740
  35.1 3.5 %collective-permute-start.3 = (bf16[2,3,192,128]{3,2,1,0:T(8,128)(2,1)S(1)}, bf16[2,3,192,128]{3,2,1,0:T(8,128)(2,1)S(1)}, u32[]{:S(2)}, u32[]{:S(2)}) collective-permute-start(bf16[2,3,192,128]{3,2,1,0:T(8,128)(2,1)S(1)} %fusion.9), channel_id=1, source_target_pairs={{1,0},{2,1},{3,2},{5,4},{6,5},{7,6},{9,8},{10,9},{11,10},{13,12},{... | collective-permute-start | bytes 884744 | tf_op jit(solution)/shard_map/ppermute | solution.py:12
  38.6 16.1 %collective-permute-start.4 = (bf16[4,1,192,128]{3,2,1,0:T(8,128)(2,1)S(1)}, bf16[4,1,192,128]{3,2,1,0:T(8,128)(2,1)S(1)}, u32[]{:S(2)}, u32[]{:S(2)}) collective-permute-start(bf16[4,1,192,128]{3,2,1,0:T(8,128)(2,1)S(1)} %get-tuple-element.18), channel_id=1, source_target_pairs={{0,4},{4,8},{8,12},{12,16},{16,20},{20,24},{24,28},{1,5},{5,9},{9,... | collective-permute-start | bytes 589832 | tf_op jit(solution)/shard_map/ppermute | solution.py:22
  42.9 11.8 %collective-permute-start.5 = (bf16[4,1,192,128]{3,2,1,0:T(8,128)(2,1)S(1)}, bf16[4,1,192,128]{3,2,1,0:T(8,128)(2,1)S(1)}, u32[]{:S(2)}, u32[]{:S(2)}) collective-permute-start(bf16[4,1,192,128]{3,2,1,0:T(8,128)(2,1)S(1)} %get-tuple-element.19), channel_id=1, source_target_pairs={{4,0},{8,4},{12,8},{16,12},{20,16},{24,20},{28,24},{5,1},{9,5},{13... | collective-permute-start | bytes 589832 | tf_op jit(solution)/shard_map/ppermute | solution.py:23
  47.7 30.1 %collective-permute-start.10 = (bf16[3,4,1,192,128]{4,3,2,1,0:T(8,128)(2,1)}, bf16[3,4,1,192,128]{4,3,2,1,0:T(8,128)(2,1)}, u32[]{:S(2)}, u32[]{:S(2)}) collective-permute-start(bf16[3,4,1,192,128]{4,3,2,1,0:T(8,128)(2,1)} %get-tuple-element.10), channel_id=1, source_target_pairs={{0,4},{4,8},{8,12},{12,16},{16,20},{20,24},{24,28},{1,5},{5,9},{9,... | collective-permute-start | bytes 1769480 | tf_op jit(solution)/shard_map/ppermute | solution.py:22
  53.4 24.4 %collective-permute-start.11 = (bf16[3,4,1,192,128]{4,3,2,1,0:T(8,128)(2,1)}, bf16[3,4,1,192,128]{4,3,2,1,0:T(8,128)(2,1)}, u32[]{:S(2)}, u32[]{:S(2)}) collective-permute-start(bf16[3,4,1,192,128]{4,3,2,1,0:T(8,128)(2,1)} %get-tuple-element.11), channel_id=1, source_target_pairs={{4,0},{8,4},{12,8},{16,12},{20,16},{24,20},{28,24},{5,1},{9,5},{13... | collective-permute-start | bytes 1769480 | tf_op jit(solution)/shard_map/ppermute | solution.py:23
  55.3 2.5 copy-start.1
  55.3 2.5 copy-start.4
  60.1 7.3 %collective-permute-start.6 = (bf16[2,3,192,128]{3,2,1,0:T(8,128)(2,1)S(1)}, bf16[2,3,192,128]{3,2,1,0:T(8,128)(2,1)S(1)}, u32[]{:S(2)}, u32[]{:S(2)}) collective-permute-start(bf16[2,3,192,128]{3,2,1,0:T(8,128)(2,1)S(1)} %fusion.10), channel_id=1, source_target_pairs={{1,0},{2,1},{3,2},{5,4},{6,5},{7,6},{9,8},{10,9},{11,10},{13,12},{... | collective-permute-start | bytes 884744 | tf_op jit(solution)/shard_map/ppermute | solution.py:12
  67.4 34.7 %collective-permute-start.7 = (bf16[4,1,192,128]{3,2,1,0:T(8,128)(2,1)S(1)}, bf16[4,1,192,128]{3,2,1,0:T(8,128)(2,1)S(1)}, u32[]{:S(2)}, u32[]{:S(2)}) collective-permute-start(bf16[4,1,192,128]{3,2,1,0:T(8,128)(2,1)S(1)} %get-tuple-element.14), channel_id=1, source_target_pairs={{0,4},{4,8},{8,12},{12,16},{16,20},{20,24},{24,28},{1,5},{5,9},{9,... | collective-permute-start | bytes 589832 | tf_op jit(solution)/shard_map/ppermute | solution.py:22
  71.8 30.3 %collective-permute-start.8 = (bf16[4,1,192,128]{3,2,1,0:T(8,128)(2,1)S(1)}, bf16[4,1,192,128]{3,2,1,0:T(8,128)(2,1)S(1)}, u32[]{:S(2)}, u32[]{:S(2)}) collective-permute-start(bf16[4,1,192,128]{3,2,1,0:T(8,128)(2,1)S(1)} %get-tuple-element.15), channel_id=1, source_target_pairs={{4,0},{8,4},{12,8},{16,12},{20,16},{24,20},{28,24},{5,1},{9,5},{13... | collective-permute-start | bytes 589832 | tf_op jit(solution)/shard_map/ppermute | solution.py:23
Sparse Core Ops, SparseCore 0:
  117.1 158.3 all-reduce.6
where the time goes:
time: 288 us; the launch traced here: 287 us
  waiting for transfers between devices  157 us (55%)
  local copies, waits for them, and re-layouts  41.1 us (14%)
  starting transfers between devices  34.5 us (12%)
  matrix products  21.8 us (8%)
  other arithmetic  17.8 us (6%)
  between operations  15.3 us (5%)
    psum x1, waiting for transfers between devices, shards(): summed_one = lax.psum(local_term, ('ha', 'ta'))  145 us
    unnamed x166, local copies, waits for them, and re-layouts  39.6 us
    ppermute x4, starting transfers between devices, padded(): before = lax.ppermute(last, axis, up)  19.3 us
    dot_general x3, matrix products, gather_grad(): result = jnp.dot(patches, flipped, preferred_element_type=jnp.float32)  10.9 us
    dot_general x3, matrix products, shards(): lax.dot_general(patches, grad_flat, (((0,), (0,)), ((), ())), preferred_e...  10.9 us
    ppermute x4, starting transfers between devices, from_behind(): return lax.ppermute(block, axis, route)  10 us
    ppermute x4, waiting for transfers between devices, from_behind(): return lax.ppermute(block, axis, route)  6.94 us
  transfers between devices with their start and end apart: 13, of which 5 were waited for; matrix products, arithmetic and copies ran while one was open for 21% of the time, Pallas kernels for 0%

commit v1 on v0

v1 whole, which is shorter than its diff:
```python
import functools
import math

import jax
import jax.numpy as jnp
from jax import lax
from jax.experimental import pallas as pl
from jax.experimental.pallas import tpu as pltpu
from jax.sharding import PartitionSpec as P

MESH = pl.DeviceIdType.MESH
VMEM = pl.BlockSpec(memory_space=pltpu.VMEM)


def silu_slope(pre_values):
    values = pre_values.astype(jnp.float32)
    sigmoid = jax.nn.sigmoid(values)
    return sigmoid * (1.0 + values * (1.0 - sigmoid))


def exchange(ta_n, ha_n, g_ref, out_ref, send_sems, recv_sems):
    ta, ha = lax.axis_index("ta"), lax.axis_index("ha")
    frames, rows = g_ref.shape[0], g_ref.shape[1]
    has_up, has_down = ha > 0, ha < ha_n - 1
    has_earlier, has_later = ta > 0, ta < ta_n - 1
    barrier = pltpu.get_barrier_semaphore()

    def device(d_ta, d_ha):
        return (ha + d_ha, ta + d_ta)

    def copy(index, source, target, d_ta, d_ha):
        return pltpu.make_async_remote_copy(
            src_ref=source,
            dst_ref=target,
            send_sem=send_sems.at[index],
            recv_sem=recv_sems.at[index],
            device_id=device(d_ta, d_ha),
            device_id_type=MESH,
        )

    for there, d_ta, d_ha in ((has_up, 0, -1), (has_down, 0, 1), (has_later, 1, 0)):

        @pl.when(there)
        def _():
            pl.semaphore_signal(barrier, inc=1, device_id=device(d_ta, d_ha), device_id_type=MESH)

    below = copy(0, g_ref.at[:, rows - 1], out_ref.at[pl.ds(0, frames), 0], 0, 1)
    above = copy(1, g_ref.at[:, 0], out_ref.at[pl.ds(0, frames), rows + 1], 0, -1)
    earlier = copy(2, g_ref, out_ref.at[pl.ds(frames, 2), pl.ds(1, rows)], -1, 0)
    corner_top = copy(3, out_ref.at[pl.ds(0, frames), 0], out_ref.at[pl.ds(frames, 2), 0], -1, 0)
    corner_end = copy(
        4, out_ref.at[pl.ds(0, frames), rows + 1], out_ref.at[pl.ds(frames, 2), rows + 1], -1, 0
    )
    peers = has_up.astype(jnp.int32) + has_down.astype(jnp.int32) + has_earlier.astype(jnp.int32)
    pl.semaphore_wait(barrier, peers)
    pl.when(has_down)(below.start)
    pl.when(has_up)(above.start)
    pl.when(has_earlier)(earlier.start)
    zero_row = jnp.zeros((frames,) + g_ref.shape[2:], g_ref.dtype)

    @pl.when(jnp.logical_not(has_up))
    def _():
        out_ref[0:frames, 0] = zero_row
        out_ref[frames : frames + 2, 0] = zero_row

    @pl.when(jnp.logical_not(has_down))
    def _():
        out_ref[0:frames, rows + 1] = zero_row
        out_ref[frames : frames + 2, rows + 1] = zero_row

    @pl.when(jnp.logical_not(has_later))
    def _():
        for row in range(rows + 2):
            out_ref[frames : frames + 2, row] = zero_row

    out_ref[0:frames, 1 : rows + 1] = g_ref[...]

    @pl.when(has_up)
    def _():
        below.wait_recv()

        @pl.when(has_earlier)
        def _():
            corner_top.start()

    @pl.when(has_down)
    def _():
        above.wait_recv()

        @pl.when(has_earlier)
        def _():
            corner_end.start()

    @pl.when(has_later)
    def _():
        earlier.wait_recv()
        pl.when(has_up)(corner_top.wait_recv)
        pl.when(has_down)(corner_end.wait_recv)

    pl.when(has_down)(below.wait_send)
    pl.when(has_up)(above.wait_send)

    @pl.when(has_earlier)
    def _():
        earlier.wait_send()
        pl.when(has_up)(corner_top.wait_send)
        pl.when(has_down)(corner_end.wait_send)


def halo(gradient, ta_n, ha_n):
    frames, rows, cols, channels = gradient.shape
    return pl.pallas_call(
        functools.partial(exchange, ta_n, ha_n),
        out_shape=jax.ShapeDtypeStruct((frames + 2, rows + 2, cols, channels), gradient.dtype),
        in_specs=[VMEM],
        out_specs=VMEM,
        scratch_shapes=[pltpu.SemaphoreType.DMA((5,)), pltpu.SemaphoreType.DMA((5,))],
        compiler_params=pltpu.CompilerParams(collective_id=0, has_side_effects=True),
        name="halo",
    )(gradient)


def convolve(last, act, wide_ref, x_ref, pre_ref, k_ref, kg_ref, out_ref, shifted):
    frames, rows, cols, channels = x_ref.shape
    column = lax.broadcasted_iota(jnp.int32, (cols, channels), 0)
    for f in range(frames + 2):
        for r in range(rows + 2):
            line = wide_ref[f, r]
            wide = line.astype(jnp.float32)
            after = jnp.where(column < cols - 1, pltpu.roll(wide, cols - 1, 0), 0.0)
            before = jnp.where(column > 0, pltpu.roll(wide, 1, 0), 0.0)
            shifted[f, r, :, 0:channels] = after.astype(line.dtype)
            shifted[f, r, :, channels : 2 * channels] = line
            shifted[f, r, :, 2 * channels : 3 * channels] = before.astype(line.dtype)

    def window(f, a, b):
        return shifted[f + 2 - a, 2 - b : 2 - b + rows].reshape(rows * cols, 3 * channels)

    taps = [(a, b) for a in range(3) for b in range(3)]
    inputs = []
    for f in range(frames):
        values = x_ref[f].reshape(rows * cols, channels)
        if act:
            wide = values.astype(jnp.float32)
            values = (wide * jax.nn.sigmoid(wide)).astype(jnp.bfloat16)
        inputs.append(values.T)
    for a, b in taps:
        term = None
        for f in range(frames):
            part = jnp.dot(inputs[f], window(f, a, b), preferred_element_type=jnp.float32)
            term = part if term is None else term + part
        for c in range(3):
            block = term[:, c * channels : (c + 1) * channels]
            kg_ref[(a * 3 + b) * 3 + c] = block.astype(kg_ref.dtype)
    for f in range(frames):
        total = None
        for a, b in taps:
            part = jnp.dot(window(f, a, b), k_ref[a * 3 + b], preferred_element_type=jnp.float32)
            total = part if total is None else total + part
        if not last:
            total = total * silu_slope(pre_ref[f].reshape(rows * cols, channels))
        out_ref[f] = total.astype(out_ref.dtype).reshape(rows, cols, channels)


def layer(wide, saved, pre, flipped, last):
    frames, rows, cols, channels = saved.shape
    return pl.pallas_call(
        functools.partial(convolve, last, not last),
        out_shape=(
            jax.ShapeDtypeStruct((27, channels, channels), jnp.bfloat16),
            jax.ShapeDtypeStruct(saved.shape, jnp.bfloat16),
        ),
        in_specs=[VMEM] * 4,
        out_specs=(VMEM, VMEM),
        scratch_shapes=[pltpu.VMEM((frames + 2, rows + 2, cols, 3 * channels), jnp.bfloat16)],
        compiler_params=pltpu.CompilerParams(vmem_limit_bytes=40 * 1024 * 1024),
        cost_estimate=pl.CostEstimate(
            flops=4 * 27 * frames * rows * cols * channels * channels,
            bytes_accessed=5_000_000,
            transcendentals=0,
        ),
        name="layer",
    )(wide, saved, pre, flipped)


def shards(
    layer_input, pre_one, pre_two, pre_three, kernel_one, kernel_two, kernel_three, upstream
):
    frame_count, row_count, col_count, channels = layer_input.shape
    ta_n, ha_n = lax.axis_size("ta"), lax.axis_size("ha")
    cells_total = frame_count * row_count * col_count * ta_n * ha_n
    norm_scale = 1.0 / math.sqrt(cells_total)
    gradient = (upstream.astype(jnp.float32) * silu_slope(pre_three)).astype(jnp.bfloat16)
    layers = [
        (kernel_three, pre_two, False),
        (kernel_two, pre_one, False),
        (kernel_one, layer_input, True),
    ]
    reduced = []
    for kernel, saved, last in layers:
        flipped = jnp.swapaxes(kernel, 3, 4).reshape(9, 3 * channels, channels)
        term, gradient = layer(halo(gradient, ta_n, ha_n), saved, saved, flipped, last)
        term = term.reshape(3, 3, 3, channels, channels)
        piece = lax.psum_scatter(term, "ha", scatter_dimension=3, tiled=True)
        total = lax.psum(piece.astype(jnp.float32), "ta")
        reduced.append(total * norm_scale)
    return (gradient, reduced[2], reduced[1], reduced[0])


def solution(mesh):
    return jax.shard_map(
        shards,
        mesh=mesh,
        in_specs=(
            P("ta", "ha", None, None),
            P("ta", "ha", None, None),
            P("ta", "ha", None, None),
            P("ta", "ha", None, None),
            P(),
            P(),
            P(),
            P("ta", "ha", None, None),
        ),
        out_specs=(
            P("ta", "ha", None, None),
            P(None, None, None, "ha", None),
            P(None, None, None, "ha", None),
            P(None, None, None, "ha", None),
        ),
        check_vma=False,
    )
```

time: 288 us -> 247 us (0.86)
  Pallas kernels: 0 us -> 48.4 us
  starting transfers between devices: 34.5 us -> 0.12 us
  local copies, waits for them, and re-layouts: 41.1 us -> 10.1 us
  matrix products: 21.8 us -> 0 us
  blocking collectives: 0 us -> 18.4 us
  other arithmetic: 17.8 us -> 3.59 us
  waiting for transfers between devices: 157 us -> 152 us
    reduce_scatter x0 -> x3, waiting for transfers between devices: none -> 152 us  [shards(): piece = lax.psum_scatter(term, 'ha', scatter_dimension=3, tiled=True)]
    psum x1 -> x0, waiting for transfers between devices: 145 us -> none  [shards(): summed_one = lax.psum(local_term, ('ha', 'ta'))]
    pallas_call x0 -> x6, Pallas kernels: none -> 48.4 us  [the longest x3 35.2 us: halo(): pl.pallas_call(functools.partial(exchange, ta_n, ha_n), out_shape=jax.Sha...]
    ppermute x12 -> x0, starting transfers between devices: 34.5 us -> none  [the longest x4 19.3 us: padded(): before = lax.ppermute(last, axis, up)]
    unnamed x166 -> x22, local copies, waits for them, and re-layouts: 39.6 us -> 6.02 us
    dot_general x6 -> x0, matrix products: 21.8 us -> none  [the longest x3 10.9 us: gather_grad(): result = jnp.dot(patches, flipped, preferred_element_type=jnp.float32)]
    psum x0 -> x1, blocking collectives: none -> 18.4 us  [shards(): total = lax.psum(piece.astype(jnp.float32), 'ta')]
    ppermute x12 -> x0, waiting for transfers between devices: 11.6 us -> none  [the longest x4 6.94 us: from_behind(): return lax.ppermute(block, axis, route)]
  transfers between devices with their start and end apart: 13 -> 3, of which waited for: 5 -> 3; matrix products, arithmetic and copies ran while one was open for 21% -> 1% of each run, Pallas kernels for 0% -> 14%
where the time goes in v1:
time: 247 us
  waiting for transfers between devices  152 us (62%)
  Pallas kernels  48.4 us (20%)
  blocking collectives  18.4 us (7%)
  between operations  13.9 us (6%)
  local copies, waits for them, and re-layouts  10.1 us (4%)
  other arithmetic  3.59 us (1%)
    reduce_scatter x3, waiting for transfers between devices, shards(): piece = lax.psum_scatter(term, 'ha', scatter_dimension=3, tiled=True)  152 us
    pallas_call x3, Pallas kernels, halo(): pl.pallas_call(functools.partial(exchange, ta_n, ha_n), out_shape=jax.Sha...  35.2 us
    psum x1, blocking collectives, shards(): total = lax.psum(piece.astype(jnp.float32), 'ta')  18.4 us
    pallas_call x3, Pallas kernels, layer(): pl.pallas_call(functools.partial(convolve, last, not last), out_shape=(ja...  13.2 us
    unnamed x22, local copies, waits for them, and re-layouts  6.02 us
  transfers between devices with their start and end apart: 3, of which 3 were waited for; matrix products, arithmetic and copies ran while one was open for 1% of the time, Pallas kernels for 14%

profile of v1, /device:TPU:0, one launch (start us, length us, event | category | flops | bytes accessed | tf_op | source)
XLA Modules:
  0.0 247.0 jit_solution(7231033193150402274)
XLA Ops:
  7.2 0.0 copy-start.8
  7.2 0.0 reduce-scatter.8.cloned.1.call-start
  7.2 2.1 fusion.6.g_ref
  9.3 9.1 %halo.3.wide_ref = bf16[4,5,192,128]{3,2,1,0:T(8,128)(2,1)} custom-call(bf16[2,3,192,128]{3,2,1,0:T(8,128)(2,1)} %fusion.6.g_ref), custom_call_target="tpu_custom_call" | custom-call | tf_op jit(solution)/shard_map/halo/pallas_call | solution.py:112
  18.4 0.0 copy-start
  18.4 0.0 copy-done.8
  18.4 0.0 copy-start.5
  18.5 1.4 copy.12
  19.9 0.0 copy-done
  19.9 0.0 copy-done.5
  19.9 4.2 %layer.3 = (bf16[27,128,128]{2,1,0:T(8,128)(2,1)}, bf16[2,3,192,128]{3,2,1,0:T(8,128)(2,1)S(1)}) custom-call(bf16[4,5,192,128]{3,2,1,0:T(8,128)(2,1)S(1)} %copy-done, bf16[2,3,192,128]{3,2,1,0:T(8,128)(2,1)S(1)} %copy-done.5, bf16[2,3,192,128]{3,2,1,0:T(8,128)(2,1)S(1)} %copy-done.5, bf16[9,384,128]{2,1,0:T(8,128)(2,1)S(1)} %bitcast.11), custom_call_target="tpu_custom_call" | custom-call | flops 2038431744 | bytes 5000000 | tf_op jit(solution)/shard_map/layer/pallas_call | solution.py:167
  24.1 0.0 copy-start.3
  24.1 0.7 copy-done.3
  24.8 0.0 copy-start.9
  24.8 0.0 reduce-scatter.8.cloned.1.call-update
  24.8 0.0 reduce-scatter.6.cloned.1.call-start
  24.9 1.1 copy-done.9
  26.0 1.4 copy.13
  27.4 0.0 copy-start.6
  27.4 13.2 %halo.4.wide_ref = bf16[4,5,192,128]{3,2,1,0:T(8,128)(2,1)} custom-call(bf16[2,3,192,128]{3,2,1,0:T(8,128)(2,1)} %copy-done.3), custom_call_target="tpu_custom_call" | custom-call | tf_op jit(solution)/shard_map/halo/pallas_call | solution.py:112
  40.6 0.0 copy-done.6
  40.6 0.0 copy-start.1
  40.6 1.2 copy-done.1
  41.8 4.2 %layer.4 = (bf16[27,128,128]{2,1,0:T(8,128)(2,1)}, bf16[2,3,192,128]{3,2,1,0:T(8,128)(2,1)S(1)}) custom-call(bf16[4,5,192,128]{3,2,1,0:T(8,128)(2,1)S(1)} %copy-done.1, bf16[2,3,192,128]{3,2,1,0:T(8,128)(2,1)S(1)} %copy-done.6, bf16[2,3,192,128]{3,2,1,0:T(8,128)(2,1)S(1)} %copy-done.6, bf16[9,384,128]{2,1,0:T(8,128)(2,1)S(1)} %bitcast.9), custom_call_target="tpu_custom_call" | custom-call | flops 2038431744 | bytes 5000000 | tf_op jit(solution)/shard_map/layer/pallas_call | solution.py:167
  46.0 0.0 copy-start.4
  46.1 0.7 copy-done.4
  46.8 0.0 copy-start.10
  46.8 0.0 reduce-scatter.6.cloned.1.call-update
  46.8 0.0 reduce-scatter.4.cloned.1.call-start
  46.8 1.1 copy-done.10
  47.9 1.4 copy.14
  49.3 0.0 copy-start.7
  49.3 12.8 %halo.5.wide_ref = bf16[4,5,192,128]{3,2,1,0:T(8,128)(2,1)} custom-call(bf16[2,3,192,128]{3,2,1,0:T(8,128)(2,1)} %copy-done.4), custom_call_target="tpu_custom_call" | custom-call | tf_op jit(solution)/shard_map/halo/pallas_call | solution.py:112
  62.1 0.0 copy-done.7
  62.2 0.0 copy-start.2
  62.2 1.2 copy-done.2
  63.4 4.8 %layer.5 = (bf16[27,128,128]{2,1,0:T(8,128)(2,1)}, bf16[2,3,192,128]{3,2,1,0:T(8,128)(2,1)}) custom-call(bf16[4,5,192,128]{3,2,1,0:T(8,128)(2,1)S(1)} %copy-done.2, bf16[2,3,192,128]{3,2,1,0:T(8,128)(2,1)S(1)} %copy-done.7, bf16[2,3,192,128]{3,2,1,0:T(8,128)(2,1)S(1)} %copy-done.7, bf16[9,384,128]{2,1,0:T(8,128)(2,1)S(1)} %bitcast.10), custom_call_target="tpu_custom_call" | custom-call | flops 2038431744 | bytes 5000000 | tf_op jit(solution)/shard_map/layer/pallas_call | solution.py:167
  68.2 0.0 reduce-scatter.4.cloned.1.call-update
  68.2 23.7 %reduce-scatter.8.cloned.1.call-done = bf16[3,3,3,16,128]{4,3,2,1,0:T(8,128)(2,1)} async-done(((bf16[3,3,3,128,128]{4,3,2,1,0:T(8,128)(2,1)}), bf16[3,3,3,16,128]{4,3,2,1,0:T(8,128)(2,1)}) %reduce-scatter.8.cloned.1.call-update) | async-done | bytes 110608 | tf_op jit(solution)/shard_map/reduce_scatter | solution.py:204
  91.9 64.3 %reduce-scatter.6.cloned.1.call-done = bf16[3,3,3,16,128]{4,3,2,1,0:T(8,128)(2,1)} async-done(((bf16[3,3,3,128,128]{4,3,2,1,0:T(8,128)(2,1)}), bf16[3,3,3,16,128]{4,3,2,1,0:T(8,128)(2,1)}) %reduce-scatter.6.cloned.1.call-update) | async-done | bytes 110608 | tf_op jit(solution)/shard_map/reduce_scatter | solution.py:204
  156.1 64.4 %reduce-scatter.4.cloned.1.call-done = bf16[3,3,3,16,128]{4,3,2,1,0:T(8,128)(2,1)} async-done(((bf16[3,3,3,128,128]{4,3,2,1,0:T(8,128)(2,1)}), bf16[3,3,3,16,128]{4,3,2,1,0:T(8,128)(2,1)}) %reduce-scatter.4.cloned.1.call-update) | async-done | bytes 110608 | tf_op jit(solution)/shard_map/reduce_scatter | solution.py:204
  220.6 18.4 %all-reduce.2 = (f32[3,3,3,16,128]{4,3,2,1,0:T(8,128)S(1)}, f32[3,3,3,16,128]{4,3,2,1,0:T(8,128)S(1)}, f32[3,3,3,16,128]{4,3,2,1,0:T(8,128)S(1)}) all-reduce(bf16[3,3,3,16,128]{4,3,2,1,0:T(8,128)(2,1)} %reduce-scatter.4.cloned.1.call-done, ...), channel_id=1, replica_groups=mesh['ha'=8,'ta'=4] {'ta'}, use_global_device_ids=true, to_apply=%region_1.0 | all-reduce | flops 165888 | bytes 995328 | tf_op jit(solution)/shard_map/psum | solution.py:205
  238.9 0.7 broadcast_multiply_fusion.2
  239.6 0.8 broadcast_multiply_fusion
Async XLA Ops:
  7.2 11.3 %copy-start.8 = (bf16[3,3,3,128,128]{4,3,2,1,0:T(8,128)(2,1)S(1)}, bf16[3,3,3,128,128]{4,3,2,1,0:T(8,128)(2,1)}, u32[]{:S(2)}) copy-start(bf16[3,3,3,128,128]{4,3,2,1,0:T(8,128)(2,1)} %param.14) | copy-start | bytes 2654212
  7.2 84.7 %reduce-scatter.8.cloned.1.call-start = ((), (), s32[]{:S(2)}) async-start(), calls=%async_computation.5 | async-start | bytes 995328 | tf_op jit(solution)/shard_map/reduce_scatter | solution.py:204
  18.4 1.4 copy-start
  18.4 1.4 copy-start.5
  24.1 0.7 copy-start.3
  24.8 1.2 copy-start.9
  24.8 131.3 %reduce-scatter.6.cloned.1.call-start = ((), (), s32[]{:S(2)}) async-start(), calls=%async_computation.4 | async-start | bytes 995328 | tf_op jit(solution)/shard_map/reduce_scatter | solution.py:204
  27.4 13.3 %copy-start.6 = (bf16[2,3,192,128]{3,2,1,0:T(8,128)(2,1)S(1)}, bf16[2,3,192,128]{3,2,1,0:T(8,128)(2,1)}, u32[]{:S(2)}) copy-start(bf16[2,3,192,128]{3,2,1,0:T(8,128)(2,1)} %pre_ref.4) | copy-start | bytes 884740
  40.6 1.2 copy-start.1
  46.0 0.7 copy-start.4
  46.8 1.2 copy-start.10
  46.8 173.8 %reduce-scatter.4.cloned.1.call-start = ((), (), s32[]{:S(2)}) async-start(), calls=%async_computation.3 | async-start | bytes 995328 | tf_op jit(solution)/shard_map/reduce_scatter | solution.py:204
  49.3 12.8 %copy-start.7 = (bf16[2,3,192,128]{3,2,1,0:T(8,128)(2,1)S(1)}, bf16[2,3,192,128]{3,2,1,0:T(8,128)(2,1)}, u32[]{:S(2)}) copy-start(bf16[2,3,192,128]{3,2,1,0:T(8,128)(2,1)} %pre_ref.5) | copy-start | bytes 884740
  62.2 1.2 copy-start.2
Sparse Core Ops, SparseCore 0:
  25.0 66.8 reduce-scatter.7
  95.3 60.8 reduce-scatter.5
  159.5 60.9 reduce-scatter.3

commit v2 on v1

--- a/solution.py
+++ b/solution.py
@@ -137,6 +137,8 @@
         return shifted[f + 2 - a, 2 - b : 2 - b + rows].reshape(rows * cols, 3 * channels)
 
     taps = [(a, b) for a in range(3) for b in range(3)]
+    pieces = kg_ref.shape[:2] + kg_ref.shape[5:]
+    kg_ref[:, :, 1, 1, 6] = jnp.zeros(pieces, kg_ref.dtype)
     inputs = []
     for f in range(frames):
         values = x_ref[f].reshape(rows * cols, channels)
@@ -150,8 +152,9 @@
             part = jnp.dot(inputs[f], window(f, a, b), preferred_element_type=jnp.float32)
             term = part if term is None else term + part
         for c in range(3):
-            block = term[:, c * channels : (c + 1) * channels]
-            kg_ref[(a * 3 + b) * 3 + c] = block.astype(kg_ref.dtype)
+            block = term[:, c * channels : (c + 1) * channels].astype(kg_ref.dtype)
+            tap = (a * 3 + b) * 3 + c
+            kg_ref[:, :, tap // 14, tap // 7 % 2, tap % 7] = block.reshape(pieces)
     for f in range(frames):
         total = None
         for a, b in taps:
@@ -162,12 +165,14 @@
         out_ref[f] = total.astype(out_ref.dtype).reshape(rows, cols, channels)
 
 
-def layer(wide, saved, pre, flipped, last):
+def layer(wide, saved, pre, flipped, last, ha_n):
     frames, rows, cols, channels = saved.shape
     return pl.pallas_call(
         functools.partial(convolve, last, not last),
         out_shape=(
-            jax.ShapeDtypeStruct((27, channels, channels), jnp.bfloat16),
+            jax.ShapeDtypeStruct(
+                (ha_n // 2, 2, 2, 2, 7, channels // ha_n, channels), jnp.bfloat16
+            ),
             jax.ShapeDtypeStruct(saved.shape, jnp.bfloat16),
         ),
         in_specs=[VMEM] * 4,
@@ -183,6 +188,172 @@
     )(wide, saved, pre, flipped)
 
 
+def added(one, two):
+    return (one.astype(jnp.float32) + two.astype(jnp.float32)).astype(jnp.bfloat16)
+
+
+def reduce_shapes(term_shape):
+    depth, tail = term_shape[0], term_shape[4:]
+    half = depth // 2
+    shapes = [
+        (depth, 2, 2) + tail,
+        (depth, 2, 2) + tail,
+        (half, 2) + tail,
+        (half, 2) + tail,
+        (half,) + tail,
+        (half, 2) + tail,
+        (half, 2) + tail,
+        (half,) + tail,
+        (depth,) + tail,
+        (depth - 1,) + tail,
+        (4,) + tail,
+    ]
+    return [pltpu.VMEM(shape, jnp.bfloat16) for shape in shapes]
+
+
+def reduce_sems(depth):
+    return 5 + depth - 1 + 3
+
+
+def reduce_peers(depth):
+    ta, ha = lax.axis_index("ta"), lax.axis_index("ha")
+    z, x, y, core = ha // 2, ha % 2, ta // 2, ta % 2
+    across_core = (ha, y * 2 + 1 - core)
+    across_y = (ha, (1 - y) * 2 + core)
+    across_x = (z * 2 + 1 - x, ta)
+    along_z = [((z + step) % depth * 2 + x, ta) for step in range(1, depth)]
+    around = [(ha, (ta + step) % 4) for step in range(1, 4)]
+    return across_core, across_y, across_x, along_z, around
+
+
+def reduce_phases(term, out_ref, buffers, send_sems, recv_sems, scale):
+    depth = term.shape[0]
+    half = depth // 2
+    ta, ha = lax.axis_index("ta"), lax.axis_index("ha")
+    z, x, y, core = ha // 2, ha % 2, ta // 2, ta % 2
+    across_core, across_y, across_x, along_z, around = reduce_peers(depth)
+    from_core, cores, low_x, low, low_y, top_y, top, top_x, rest, from_z, whole = buffers
+
+    def copy(index, source, target, peer):
+        return pltpu.make_async_remote_copy(
+            src_ref=source,
+            dst_ref=target,
+            send_sem=send_sems.at[index],
+            recv_sem=recv_sems.at[index],
+            device_id=peer,
+            device_id_type=MESH,
+        )
+
+    core_copy = copy(0, term.at[:, :, :, 1 - core], from_core, across_core)
+    low_x_copy = copy(1, cores.at[pl.ds(0, half), 1 - x], low_x, across_x)
+    low_y_copy = copy(2, low.at[:, 1 - y], low_y, across_y)
+    top_y_copy = copy(3, cores.at[pl.ds(half, half), :, 1 - y], top_y, across_y)
+    top_x_copy = copy(4, top.at[:, 1 - x], top_x, across_x)
+    z_copies = [
+        copy(5 + step, rest.at[(z + step + 1) % depth], from_z.at[step], along_z[step])
+        for step in range(depth - 1)
+    ]
+    last_copies = [
+        copy(4 + depth + step, whole.at[ta], whole.at[ta], around[step]) for step in range(3)
+    ]
+
+    def start():
+        core_copy.start()
+
+    def first():
+        core_copy.wait_recv()
+        for row in range(half):
+            cores[row] = added(term[row, :, :, core], from_core[row])
+        low_x_copy.start()
+        for row in range(half, depth):
+            cores[row] = added(term[row, :, :, core], from_core[row])
+        top_y_copy.start()
+
+    def second():
+        low_x_copy.wait_recv()
+        low[...] = added(cores[0:half, x], low_x[...])
+        low_y_copy.start()
+        top_y_copy.wait_recv()
+        top[...] = added(cores[half:depth, :, y], top_y[...])
+        top_x_copy.start()
+
+    def third():
+        low_y_copy.wait_recv()
+        rest[0:half] = added(low[:, y], low_y[...])
+        top_x_copy.wait_recv()
+        rest[half:depth] = added(top[:, x], top_x[...])
+        for each in z_copies:
+            each.start()
+
+    def fourth():
+        total = rest[z].astype(jnp.float32)
+        for step in range(depth - 1):
+            z_copies[step].wait_recv()
+            total = total + from_z[step].astype(jnp.float32)
+        whole[ta] = total.astype(jnp.bfloat16)
+        for each in last_copies:
+            each.start()
+
+    def finish():
+        for each in last_copies:
+            each.wait_recv()
+        for tap in range(27):
+            out_ref[tap] = whole[tap // 7, tap % 7].astype(jnp.float32) * scale
+        for each in [core_copy, low_x_copy, low_y_copy, top_y_copy, top_x_copy] + z_copies + last_copies:
+            each.wait_send()
+
+    return [start, first, second, third, fourth, finish]
+
+
+def greet_reducers(depth):
+    barrier = pltpu.get_barrier_semaphore()
+    _, _, across_x, along_z, around = reduce_peers(depth)
+    peers = [across_x] + along_z + around
+    for peer in peers:
+        pl.semaphore_signal(barrier, inc=1, device_id=peer, device_id_type=MESH)
+    pl.semaphore_wait(barrier, len(peers))
+
+
+def reducer(scale, count, *refs):
+    terms, outs = refs[:count], refs[count : 2 * count]
+    buffers = refs[2 * count : -2]
+    send_sems, recv_sems = refs[-2:]
+    greet_reducers(terms[0].shape[0])
+    each = len(buffers) // count
+    stages = [
+        reduce_phases(
+            terms[n],
+            outs[n],
+            buffers[n * each : (n + 1) * each],
+            send_sems.at[n],
+            recv_sems.at[n],
+            scale,
+        )
+        for n in range(count)
+    ]
+    for turn in range(len(stages[0]) + count - 1):
+        for n in range(count):
+            if 0 <= turn - n < len(stages[0]):
+                stages[n][turn - n]()
+
+
+def reduce_terms(terms, scale):
+    count, shape = len(terms), terms[0].shape
+    sems = reduce_sems(shape[0])
+    return pl.pallas_call(
+        functools.partial(reducer, scale, count),
+        out_shape=[jax.ShapeDtypeStruct((27,) + shape[5:], jnp.float32)] * count,
+        in_specs=[VMEM] * count,
+        out_specs=[VMEM] * count,
+        scratch_shapes=reduce_shapes(shape) * count
+        + [pltpu.SemaphoreType.DMA((count, sems)), pltpu.SemaphoreType.DMA((count, sems))],
+        compiler_params=pltpu.CompilerParams(
+            collective_id=1, has_side_effects=True, vmem_limit_bytes=48 * 1024 * 1024
+        ),
+        name="reduce",
+    )(*terms)
+
+
 def shards(
     layer_input, pre_one, pre_two, pre_three, kernel_one, kernel_two, kernel_three, upstream
 ):
@@ -196,14 +367,13 @@
         (kernel_two, pre_one, False),
         (kernel_one, layer_input, True),
     ]
-    reduced = []
+    terms = []
     for kernel, saved, last in layers:
         flipped = jnp.swapaxes(kernel, 3, 4).reshape(9, 3 * channels, channels)
-        term, gradient = layer(halo(gradient, ta_n, ha_n), saved, saved, flipped, last)
-        term = term.reshape(3, 3, 3, channels, channels)
-        piece = lax.psum_scatter(term, "ha", scatter_dimension=3, tiled=True)
-        total = lax.psum(piece.astype(jnp.float32), "ta")
-        reduced.append(total * norm_scale)
+        term, gradient = layer(halo(gradient, ta_n, ha_n), saved, saved, flipped, last, ha_n)
+        terms.append(term)
+    reduced = reduce_terms(terms, norm_scale)
+    reduced = [total.reshape(3, 3, 3, channels // ha_n, channels) for total in reduced]
     return (gradient, reduced[2], reduced[1], reduced[0])
 
 

time: 247 us -> 97.4 us (0.39)
  waiting for transfers between devices: 152 us -> 0 us
  Pallas kernels: 48.4 us -> 81.2 us
  blocking collectives: 18.4 us -> 0 us
  between operations: 13.9 us -> 0.79 us
  local copies, waits for them, and re-layouts: 10.1 us -> 12.9 us
    reduce_scatter x3 -> x0, waiting for transfers between devices: 152 us -> none  [shards(): piece = lax.psum_scatter(term, 'ha', scatter_dimension=3, tiled=True)]
    pallas_call x0 -> x1, Pallas kernels: none -> 34.4 us  [reduce_terms(): pl.pallas_call(functools.partial(reducer, scale, count), out_shape=[jax.S...]
    psum x1 -> x0, blocking collectives: 18.4 us -> none  [shards(): total = lax.psum(piece.astype(jnp.float32), 'ta')]
    unnamed x22 -> x29, local copies, waits for them, and re-layouts: 6.02 us -> 8.23 us
  transfers between devices with their start and end apart: 3 -> 0, of which waited for: 3 -> 0; matrix products, arithmetic and copies ran while one was open for 1% -> 0% of each run, Pallas kernels for 14% -> 0%
where the time goes in v2:
time: 97.4 us; the launch traced here: 97 us
  Pallas kernels  81.2 us (83%)
  local copies, waits for them, and re-layouts  12.9 us (13%)
  other arithmetic  2.09 us (2%)
    pallas_call x1, Pallas kernels, reduce_terms(): pl.pallas_call(functools.partial(reducer, scale, count), out_shape=[jax.S...  34.4 us
    pallas_call x3, Pallas kernels, halo(): pl.pallas_call(functools.partial(exchange, ta_n, ha_n), out_shape=jax.Sha...  33.7 us
    pallas_call x3, Pallas kernels, layer(): pl.pallas_call(functools.partial(convolve, last, not last), out_shape=(ja...  13.2 us
    unnamed x29, local copies, waits for them, and re-layouts  8.23 us
    transpose x3, local copies, waits for them, and re-layouts, shards(): flipped = jnp.swapaxes(kernel, 3, 4).reshape(9, 3 * channels, channels)  4.7 us
    convert_element_type x1, other arithmetic, shards(): (upstream.astype(jnp.float32) * silu_slope(pre_three)).astype(jnp.bfloat16)  2.09 us

profile of v2, /device:TPU:0, one launch (start us, length us, event | category | flops | bytes accessed | tf_op | source)
XLA Modules:
  0.0 97.0 jit_solution(6803480037514647549)
XLA Ops:
  0.6 0.0 copy-start.10
  0.6 2.1 %fusion.6.g_ref = bf16[2,3,192,128]{3,2,1,0:T(8,128)(2,1)} fusion(bf16[2,3,192,128]{3,2,1,0:T(8,128)(2,1)} %param.11, bf16[2,3,192,128]{3,2,1,0:T(8,128)(2,1)} %param.15), kind=kLoop, calls=%fused_computation.8 | loop fusion | flops 1622016 | bytes 884736 | tf_op jit(solution)/shard_map/convert_element_type | solution.py:364
  2.7 9.1 %halo.3.wide_ref = bf16[4,5,192,128]{3,2,1,0:T(8,128)(2,1)} custom-call(bf16[2,3,192,128]{3,2,1,0:T(8,128)(2,1)} %fusion.6.g_ref), custom_call_target="tpu_custom_call" | custom-call | tf_op jit(solution)/shard_map/halo/pallas_call | solution.py:112
  11.9 0.0 copy-done.10
  11.9 0.0 copy-start.11
  11.9 1.4 %copy.14 = bf16[3,3,3,128,128]{4,3,2,1,0:T(8,128)(2,1)S(1)} copy(bf16[3,3,3,128,128]{3,4,2,1,0:T(8,128)(2,1)S(1)} %bitcast.15) | data formatting | bytes 1769472 | tf_op jit(solution)/shard_map/transpose | solution.py:372
  13.3 0.0 copy-done.11
  13.3 0.0 copy-start.12
  13.3 1.7 %copy.13 = bf16[3,3,3,128,128]{4,3,2,1,0:T(8,128)(2,1)} copy(bf16[3,3,3,128,128]{3,4,2,1,0:T(8,128)(2,1)S(1)} %bitcast.16) | data formatting | bytes 1769472 | tf_op jit(solution)/shard_map/transpose | solution.py:372
  15.0 0.0 copy-start
  15.0 0.0 copy-done.12
  15.0 0.0 copy-start.7
  15.0 1.7 %copy.12 = bf16[3,3,3,128,128]{4,3,2,1,0:T(8,128)(2,1)} copy(bf16[3,3,3,128,128]{3,4,2,1,0:T(8,128)(2,1)S(1)} %bitcast.17) | data formatting | bytes 1769472 | tf_op jit(solution)/shard_map/transpose | solution.py:372
  16.6 0.0 copy-done
  16.6 0.0 copy-done.7
  16.6 0.0 copy-start.4
  16.6 1.2 %copy-done.4 = bf16[3,3,3,128,128]{4,3,2,1,0:T(8,128)(2,1)S(1)} copy-done((bf16[3,3,3,128,128]{4,3,2,1,0:T(8,128)(2,1)S(1)}, bf16[3,3,3,128,128]{4,3,2,1,0:T(8,128)(2,1)}, u32[]{:S(2)}) %copy-start.4) | copy-done | bytes 884760
  17.8 4.2 %layer.3 = (bf16[4,2,2,2,7,16,128]{6,5,4,3,2,1,0:T(8,128)(2,1)S(1)}, bf16[2,3,192,128]{3,2,1,0:T(8,128)(2,1)S(1)}) custom-call(bf16[4,5,192,128]{3,2,1,0:T(8,128)(2,1)S(1)} %copy-done, bf16[2,3,192,128]{3,2,1,0:T(8,128)(2,1)S(1)} %copy-done.7, bf16[2,3,192,128]{3,2,1,0:T(8,128)(2,1)S(1)} %copy-done.7, bf16[9,384,128]{2,1,0:T(8,128)(2,1)S(1)} %bitcast.11), custom_call_target="tpu_custom_call" | custom-call | flops 2038431744 | bytes 5000000 | tf_op jit(solution)/shard_map/layer/pallas_call | solution.py:170
  22.0 0.0 copy-start.5
  22.0 0.7 copy-done.5
  22.8 0.0 copy-start.8
  22.8 13.1 %halo.4.wide_ref = bf16[4,5,192,128]{3,2,1,0:T(8,128)(2,1)} custom-call(bf16[2,3,192,128]{3,2,1,0:T(8,128)(2,1)} %copy-done.5), custom_call_target="tpu_custom_call" | custom-call | tf_op jit(solution)/shard_map/halo/pallas_call | solution.py:112
  35.9 0.0 copy-done.8
  35.9 0.0 copy-start.1
  35.9 1.2 %copy-done.1 = bf16[4,5,192,128]{3,2,1,0:T(8,128)(2,1)S(1)} copy-done((bf16[4,5,192,128]{3,2,1,0:T(8,128)(2,1)S(1)}, bf16[4,5,192,128]{3,2,1,0:T(8,128)(2,1)}, u32[]{:S(2)}) %copy-start.1) | copy-done | bytes 983064
  37.1 0.0 copy-start.3
  37.1 1.2 %copy-done.3 = bf16[3,3,3,128,128]{4,3,2,1,0:T(8,128)(2,1)S(1)} copy-done((bf16[3,3,3,128,128]{4,3,2,1,0:T(8,128)(2,1)S(1)}, bf16[3,3,3,128,128]{4,3,2,1,0:T(8,128)(2,1)}, u32[]{:S(2)}) %copy-start.3) | copy-done | bytes 884760
  38.3 4.2 %layer.4 = (bf16[4,2,2,2,7,16,128]{6,5,4,3,2,1,0:T(8,128)(2,1)S(1)}, bf16[2,3,192,128]{3,2,1,0:T(8,128)(2,1)S(1)}) custom-call(bf16[4,5,192,128]{3,2,1,0:T(8,128)(2,1)S(1)} %copy-done.1, bf16[2,3,192,128]{3,2,1,0:T(8,128)(2,1)S(1)} %copy-done.8, bf16[2,3,192,128]{3,2,1,0:T(8,128)(2,1)S(1)} %copy-done.8, bf16[9,384,128]{2,1,0:T(8,128)(2,1)S(1)} %bitcast.10), custom_call_target="tpu_custom_call" | custom-call | flops 2038431744 | bytes 5000000 | tf_op jit(solution)/shard_map/layer/pallas_call | solution.py:170
  42.5 0.0 copy-start.6
  42.5 0.7 copy-done.6
  43.2 0.0 copy-start.9
  43.2 11.4 %halo.5.wide_ref = bf16[4,5,192,128]{3,2,1,0:T(8,128)(2,1)} custom-call(bf16[2,3,192,128]{3,2,1,0:T(8,128)(2,1)} %copy-done.6), custom_call_target="tpu_custom_call" | custom-call | tf_op jit(solution)/shard_map/halo/pallas_call | solution.py:112
  54.6 0.0 copy-done.9
  54.6 0.0 copy-start.2
  54.6 1.2 %copy-done.2 = bf16[4,5,192,128]{3,2,1,0:T(8,128)(2,1)S(1)} copy-done((bf16[4,5,192,128]{3,2,1,0:T(8,128)(2,1)S(1)}, bf16[4,5,192,128]{3,2,1,0:T(8,128)(2,1)}, u32[]{:S(2)}) %copy-start.2) | copy-done | bytes 983064
  55.8 4.8 %layer.5 = (bf16[4,2,2,2,7,16,128]{6,5,4,3,2,1,0:T(8,128)(2,1)S(1)}, bf16[2,3,192,128]{3,2,1,0:T(8,128)(2,1)}) custom-call(bf16[4,5,192,128]{3,2,1,0:T(8,128)(2,1)S(1)} %copy-done.2, bf16[2,3,192,128]{3,2,1,0:T(8,128)(2,1)S(1)} %copy-done.9, bf16[2,3,192,128]{3,2,1,0:T(8,128)(2,1)S(1)} %copy-done.9, bf16[9,384,128]{2,1,0:T(8,128)(2,1)S(1)} %bitcast.9), custom_call_target="tpu_custom_call" | custom-call | flops 2038431744 | bytes 5000000 | tf_op jit(solution)/shard_map/layer/pallas_call | solution.py:170
  60.6 34.4 %reduce.1 = (f32[27,16,128]{2,1,0:T(8,128)S(1)}, f32[27,16,128]{2,1,0:T(8,128)S(1)}, f32[27,16,128]{2,1,0:T(8,128)S(1)}) custom-call(bf16[4,2,2,2,7,16,128]{6,5,4,3,2,1,0:T(8,128)(2,1)S(1)} %get-tuple-element.16.refs_0_, bf16[4,2,2,2,7,16,128]{6,5,4,3,2,1,0:T(8,128)(2,1)S(1)} %get-tuple-element.17.refs_1_, ...), custom_call_target="tpu_custom_call" | custom-call | tf_op jit(solution)/shard_map/reduce/pallas_call | solution.py:343
  95.0 0.7 copy.18
  95.7 0.7 copy.19
  96.4 0.7 copy.20
Async XLA Ops:
  0.6 11.2 %copy-start.10 = (bf16[3,3,3,128,128]{4,3,2,1,0:T(8,128)(2,1)S(1)}, bf16[3,3,3,128,128]{4,3,2,1,0:T(8,128)(2,1)}, u32[]{:S(2)}) copy-start(bf16[3,3,3,128,128]{4,3,2,1,0:T(8,128)(2,1)} %param.12) | copy-start | bytes 2654212
  11.9 1.4 %copy-start.11 = (bf16[3,3,3,128,128]{4,3,2,1,0:T(8,128)(2,1)S(1)}, bf16[3,3,3,128,128]{4,3,2,1,0:T(8,128)(2,1)}, u32[]{:S(2)}) copy-start(bf16[3,3,3,128,128]{4,3,2,1,0:T(8,128)(2,1)} %param.13) | copy-start | bytes 2654212
  13.3 1.7 %copy-start.12 = (bf16[3,3,3,128,128]{4,3,2,1,0:T(8,128)(2,1)S(1)}, bf16[3,3,3,128,128]{4,3,2,1,0:T(8,128)(2,1)}, u32[]{:S(2)}) copy-start(bf16[3,3,3,128,128]{4,3,2,1,0:T(8,128)(2,1)} %param.14) | copy-start | bytes 2654212
  15.0 1.7 %copy-start = (bf16[4,5,192,128]{3,2,1,0:T(8,128)(2,1)S(1)}, bf16[4,5,192,128]{3,2,1,0:T(8,128)(2,1)}, u32[]{:S(2)}) copy-start(bf16[4,5,192,128]{3,2,1,0:T(8,128)(2,1)} %halo.3.wide_ref) | copy-start | bytes 2949124
  15.0 1.7 %copy-start.7 = (bf16[2,3,192,128]{3,2,1,0:T(8,128)(2,1)S(1)}, bf16[2,3,192,128]{3,2,1,0:T(8,128)(2,1)}, u32[]{:S(2)}) copy-start(bf16[2,3,192,128]{3,2,1,0:T(8,128)(2,1)} %pre_ref.3) | copy-start | bytes 884740
  16.6 1.2 %copy-start.4 = (bf16[3,3,3,128,128]{4,3,2,1,0:T(8,128)(2,1)S(1)}, bf16[3,3,3,128,128]{4,3,2,1,0:T(8,128)(2,1)}, u32[]{:S(2)}) copy-start(bf16[3,3,3,128,128]{4,3,2,1,0:T(8,128)(2,1)} %copy.12) | copy-start | bytes 2654212
  22.0 0.7 copy-start.5
  22.8 13.2 %copy-start.8 = (bf16[2,3,192,128]{3,2,1,0:T(8,128)(2,1)S(1)}, bf16[2,3,192,128]{3,2,1,0:T(8,128)(2,1)}, u32[]{:S(2)}) copy-start(bf16[2,3,192,128]{3,2,1,0:T(8,128)(2,1)} %pre_ref.4) | copy-start | bytes 884740
  35.9 1.2 %copy-start.1 = (bf16[4,5,192,128]{3,2,1,0:T(8,128)(2,1)S(1)}, bf16[4,5,192,128]{3,2,1,0:T(8,128)(2,1)}, u32[]{:S(2)}) copy-start(bf16[4,5,192,128]{3,2,1,0:T(8,128)(2,1)} %halo.4.wide_ref) | copy-start | bytes 2949124
  37.1 1.2 %copy-start.3 = (bf16[3,3,3,128,128]{4,3,2,1,0:T(8,128)(2,1)S(1)}, bf16[3,3,3,128,128]{4,3,2,1,0:T(8,128)(2,1)}, u32[]{:S(2)}) copy-start(bf16[3,3,3,128,128]{4,3,2,1,0:T(8,128)(2,1)} %copy.13) | copy-start | bytes 2654212
  42.5 0.7 copy-start.6
  43.2 11.4 %copy-start.9 = (bf16[2,3,192,128]{3,2,1,0:T(8,128)(2,1)S(1)}, bf16[2,3,192,128]{3,2,1,0:T(8,128)(2,1)}, u32[]{:S(2)}) copy-start(bf16[2,3,192,128]{3,2,1,0:T(8,128)(2,1)} %pre_ref.5) | copy-start | bytes 884740
  54.6 1.2 %copy-start.2 = (bf16[4,5,192,128]{3,2,1,0:T(8,128)(2,1)S(1)}, bf16[4,5,192,128]{3,2,1,0:T(8,128)(2,1)}, u32[]{:S(2)}) copy-start(bf16[4,5,192,128]{3,2,1,0:T(8,128)(2,1)} %halo.5.wide_ref) | copy-start | bytes 2949124

commit v3 on v2

v3 whole, which is shorter than its diff:
```python
import functools
import math

import jax
import jax.numpy as jnp
from jax import lax
from jax.experimental import pallas as pl
from jax.experimental.pallas import tpu as pltpu
from jax.sharding import PartitionSpec as P

MESH = pl.DeviceIdType.MESH
VMEM = pl.BlockSpec(memory_space=pltpu.VMEM)


def silu_slope(pre_values):
    values = pre_values.astype(jnp.float32)
    sigmoid = jax.nn.sigmoid(values)
    return sigmoid * (1.0 + values * (1.0 - sigmoid))


def halo_stages(ta_n, ha_n, wide, send_sems, recv_sems):
    ta, ha = lax.axis_index("ta"), lax.axis_index("ha")
    frames, rows = wide.shape[0] - 2, wide.shape[1] - 2
    has_up, has_down = ha > 0, ha < ha_n - 1
    has_earlier, has_later = ta > 0, ta < ta_n - 1

    def copy(index, source, target, d_ta, d_ha):
        return pltpu.make_async_remote_copy(
            src_ref=source,
            dst_ref=target,
            send_sem=send_sems.at[index],
            recv_sem=recv_sems.at[index],
            device_id=(ha + d_ha, ta + d_ta),
            device_id_type=MESH,
        )

    now, ahead = pl.ds(0, frames), pl.ds(frames, 2)
    below = copy(0, wide.at[now, rows], wide.at[now, 0], 0, 1)
    above = copy(1, wide.at[now, 1], wide.at[now, rows + 1], 0, -1)
    earlier = copy(2, wide.at[now, pl.ds(1, rows)], wide.at[ahead, pl.ds(1, rows)], -1, 0)
    corner_top = copy(3, wide.at[now, 0], wide.at[ahead, 0], -1, 0)
    corner_end = copy(4, wide.at[now, rows + 1], wide.at[ahead, rows + 1], -1, 0)

    def clear():
        zero_row = jnp.zeros((frames,) + wide.shape[2:], wide.dtype)

        @pl.when(jnp.logical_not(has_up))
        def _():
            wide[0:frames, 0] = zero_row
            wide[frames : frames + 2, 0] = zero_row

        @pl.when(jnp.logical_not(has_down))
        def _():
            wide[0:frames, rows + 1] = zero_row
            wide[frames : frames + 2, rows + 1] = zero_row

        @pl.when(jnp.logical_not(has_later))
        def _():
            for row in range(rows + 2):
                wide[frames : frames + 2, row] = zero_row

    def start():
        pl.when(has_down)(below.start)
        pl.when(has_up)(above.start)
        pl.when(has_earlier)(earlier.start)

    def corners():
        @pl.when(has_up)
        def _():
            below.wait_recv()
            pl.when(has_earlier)(corner_top.start)

        @pl.when(has_down)
        def _():
            above.wait_recv()
            pl.when(has_earlier)(corner_end.start)

    def arrive():
        @pl.when(has_later)
        def _():
            earlier.wait_recv()
            pl.when(has_up)(corner_top.wait_recv)
            pl.when(has_down)(corner_end.wait_recv)

    def finish():
        pl.when(has_down)(below.wait_send)
        pl.when(has_up)(above.wait_send)

        @pl.when(has_earlier)
        def _():
            earlier.wait_send()
            pl.when(has_up)(corner_top.wait_send)
            pl.when(has_down)(corner_end.wait_send)

    return clear, start, corners, arrive, finish


def shift(wide, shifted, f, first, count):
    cols, channels = wide.shape[2:]
    size = count * cols
    column = lax.broadcasted_iota(jnp.int32, (count, cols, channels), 1).reshape(size, channels)
    lines = wide[f, first : first + count]
    flat = lines.reshape(size, channels).astype(jnp.float32)
    after = jnp.where(column < cols - 1, pltpu.roll(flat, size - 1, 0), 0.0)
    before = jnp.where(column > 0, pltpu.roll(flat, 1, 0), 0.0)
    for place, values in ((0, after.astype(lines.dtype)), (2, before.astype(lines.dtype))):
        shifted[f, first : first + count, :, place * channels : (place + 1) * channels] = (
            values.reshape(lines.shape)
        )
    shifted[f, first : first + count, :, channels : 2 * channels] = lines


TAPS = [(a, b) for a in range(3) for b in range(3)]


def window(shifted, f, a, b):
    rows, cols, width = shifted.shape[1] - 2, shifted.shape[2], shifted.shape[3]
    return shifted[f + 2 - a, 2 - b : 2 - b + rows].reshape(rows * cols, width)


def kernel_term(turned, shifted, term):
    channels = turned.shape[1]
    pieces = term.shape[:2] + term.shape[5:]
    term[:, :, 1, 1, 6] = jnp.zeros(pieces, term.dtype)
    for a, b in TAPS:
        total = None
        for f in range(turned.shape[0]):
            part = jnp.dot(turned[f], window(shifted, f, a, b), preferred_element_type=jnp.float32)
            total = part if total is None else total + part
        for c in range(3):
            block = total[:, c * channels : (c + 1) * channels].astype(term.dtype)
            tap = (a * 3 + b) * 3 + c
            term[:, :, tap // 14, tap // 7 % 2, tap % 7] = block.reshape(pieces)


def back(shifted, flipped, f):
    total = None
    for a, b in TAPS:
        part = jnp.dot(
            window(shifted, f, a, b), flipped[a * 3 + b], preferred_element_type=jnp.float32
        )
        total = part if total is None else total + part
    return total


def added(one, two):
    return (one.astype(jnp.float32) + two.astype(jnp.float32)).astype(jnp.bfloat16)


def reduce_shapes(term_shape):
    depth, tail = term_shape[0], term_shape[4:]
    half = depth // 2
    shapes = [
        (depth, 2, 2) + tail,
        (depth, 2, 2) + tail,
        (half, 2) + tail,
        (half, 2) + tail,
        (half,) + tail,
        (half, 2) + tail,
        (half, 2) + tail,
        (half,) + tail,
        (depth,) + tail,
        (depth - 1,) + tail,
        (4,) + tail,
    ]
    return [pltpu.VMEM(shape, jnp.bfloat16) for shape in shapes]


def reduce_sems(depth):
    return 5 + depth - 1 + 3


def reduce_peers(depth):
    ta, ha = lax.axis_index("ta"), lax.axis_index("ha")
    z, x, y, core = ha // 2, ha % 2, ta // 2, ta % 2
    across_core = (ha, y * 2 + 1 - core)
    across_y = (ha, (1 - y) * 2 + core)
    across_x = (z * 2 + 1 - x, ta)
    along_z = [((z + step) % depth * 2 + x, ta) for step in range(1, depth)]
    around = [(ha, (ta + step) % 4) for step in range(1, 4)]
    return across_core, across_y, across_x, along_z, around


def reduce_phases(term, out_ref, buffers, send_sems, recv_sems, scale):
    depth = term.shape[0]
    half = depth // 2
    ta, ha = lax.axis_index("ta"), lax.axis_index("ha")
    z, x, y, core = ha // 2, ha % 2, ta // 2, ta % 2
    across_core, across_y, across_x, along_z, around = reduce_peers(depth)
    from_core, cores, low_x, low, low_y, top_y, top, top_x, rest, from_z, whole = buffers

    def copy(index, source, target, peer):
        return pltpu.make_async_remote_copy(
            src_ref=source,
            dst_ref=target,
            send_sem=send_sems.at[index],
            recv_sem=recv_sems.at[index],
            device_id=peer,
            device_id_type=MESH,
        )

    core_copy = copy(0, term.at[:, :, :, 1 - core], from_core, across_core)
    low_x_copy = copy(1, cores.at[pl.ds(0, half), 1 - x], low_x, across_x)
    low_y_copy = copy(2, low.at[:, 1 - y], low_y, across_y)
    top_y_copy = copy(3, cores.at[pl.ds(half, half), :, 1 - y], top_y, across_y)
    top_x_copy = copy(4, top.at[:, 1 - x], top_x, across_x)
    z_copies = [
        copy(5 + step, rest.at[(z + step + 1) % depth], from_z.at[step], along_z[step])
        for step in range(depth - 1)
    ]
    last_copies = [
        copy(4 + depth + step, whole.at[ta], whole.at[ta], around[step]) for step in range(3)
    ]

    def start():
        core_copy.start()

    def first():
        core_copy.wait_recv()
        for row in range(half):
            cores[row] = added(term[row, :, :, core], from_core[row])
        low_x_copy.start()
        for row in range(half, depth):
            cores[row] = added(term[row, :, :, core], from_core[row])
        top_y_copy.start()

    def second():
        low_x_copy.wait_recv()
        low[...] = added(cores[0:half, x], low_x[...])
        low_y_copy.start()
        top_y_copy.wait_recv()
        top[...] = added(cores[half:depth, :, y], top_y[...])
        top_x_copy.start()

    def third():
        low_y_copy.wait_recv()
        rest[0:half] = added(low[:, y], low_y[...])
        top_x_copy.wait_recv()
        rest[half:depth] = added(top[:, x], top_x[...])
        for each in z_copies:
            each.start()

    def fourth():
        total = rest[z].astype(jnp.float32)
        for step in range(depth - 1):
            z_copies[step].wait_recv()
            total = total + from_z[step].astype(jnp.float32)
        whole[ta] = total.astype(jnp.bfloat16)
        for each in last_copies:
            each.start()

    def finish():
        for each in last_copies:
            each.wait_recv()
        for tap in range(27):
            out_ref[tap] = whole[tap // 7, tap % 7].astype(jnp.float32) * scale
        for each in [core_copy, low_x_copy, low_y_copy, top_y_copy, top_x_copy] + z_copies + last_copies:
            each.wait_send()

    return [start, first, second, third, fourth, finish]


def greet(ha_n):
    barrier = pltpu.get_barrier_semaphore()
    ta, ha = lax.axis_index("ta"), lax.axis_index("ha")
    _, _, across_x, along_z, around = reduce_peers(ha_n // 2)
    peers = [across_x] + along_z + around
    for peer in peers:
        pl.semaphore_signal(barrier, inc=1, device_id=peer, device_id_type=MESH)
    other = ha - 1 + ha % 2 * 2
    exists = jnp.logical_and(other >= 0, other < ha_n)

    @pl.when(exists)
    def _():
        pl.semaphore_signal(barrier, inc=1, device_id=(other, ta), device_id_type=MESH)

    pl.semaphore_wait(barrier, len(peers) + exists.astype(jnp.int32))


def whole_kernel(ta_n, ha_n, scale, *refs):
    upstream, pre_three, saved_hbm, kernels_hbm = refs[0], refs[1], refs[2:5], refs[5:8]
    input_gradient, outs = refs[8], refs[9:12]
    saved, kernels, wides, terms = refs[12:15], refs[15:18], refs[18:21], refs[21:24]
    shifted, flipped, turned, slopes = refs[24:28]
    load_sems, halo_send, halo_recv, send_sems, recv_sems = refs[-5:]
    buffers = refs[28:-5]
    each = len(buffers) // 3
    frames, rows, cols, channels = upstream.shape
    size = rows * cols

    loads = [
        pltpu.make_async_copy(source, target, load_sems.at[n])
        for n, (source, target) in enumerate(
            zip(tuple(saved_hbm) + tuple(kernels_hbm), tuple(saved) + tuple(kernels))
        )
    ]
    for n in (0, 3, 1, 4, 2, 5):
        loads[n].start()
    halos = [
        halo_stages(ta_n, ha_n, wides[n], halo_send.at[n], halo_recv.at[n]) for n in range(3)
    ]
    sums = [
        reduce_phases(
            terms[n], outs[n], buffers[n * each : (n + 1) * each], send_sems.at[n], recv_sems.at[n], scale
        )
        for n in range(3)
    ]
    for f in range(frames):
        values = upstream[f].astype(jnp.float32) * silu_slope(pre_three[f])
        wides[0][f, 1 : rows + 1] = values.astype(jnp.bfloat16)
    greet(ha_n)
    halos[0][1]()
    for clear, _, _, _, _ in halos:
        clear()

    for n in range(3):
        _, _, corners, arrive, _ = halos[n]
        if n > 0:
            kernel_term(turned, shifted, terms[n - 1])
            sums[n - 1][0]()
        if n > 1:
            sums[n - 2][2]()
        loads[n].wait()
        loads[3 + n].wait()
        for f in range(frames):
            values = saved[n][f].reshape(size, channels)
            if n < 2:
                slopes[f] = silu_slope(values)
                wide = values.astype(jnp.float32)
                values = (wide * jax.nn.sigmoid(wide)).astype(jnp.bfloat16)
            turned[f] = values.T
        for a, b in TAPS:
            for c in range(3):
                flipped[a * 3 + b, c * channels : (c + 1) * channels] = kernels[n][a, b, c].T
        for f in range(frames):
            shift(wides[n], shifted, f, 1, rows)
        corners()
        for f in range(frames):
            shift(wides[n], shifted, f, 0, 1)
            shift(wides[n], shifted, f, rows + 1, 1)
        if n > 1:
            sums[n - 2][3]()
        arrive()
        if n > 0:
            sums[n - 1][1]()
        for f in range(frames, frames + 2):
            shift(wides[n], shifted, f, 0, rows + 2)
        if n == 2:
            kernel_term(turned, shifted, terms[n])
            sums[n][0]()
        for f in range(frames):
            total = back(shifted, flipped, f)
            if n < 2:
                total = total * slopes[f]
                wides[n + 1][f, 1 : rows + 1] = total.astype(jnp.bfloat16).reshape(
                    rows, cols, channels
                )
            else:
                input_gradient[f] = total.astype(jnp.bfloat16).reshape(rows, cols, channels)
                if f == 0:
                    sums[n][1]()
                    sums[n - 1][2]()
        if n < 2:
            halos[n + 1][1]()
    sums[0][4]()
    sums[2][2]()
    sums[1][3]()
    sums[2][3]()
    sums[1][4]()
    sums[2][4]()
    sums[0][5]()
    sums[1][5]()
    sums[2][5]()
    for halo in halos:
        halo[4]()


def shards(
    layer_input, pre_one, pre_two, pre_three, kernel_one, kernel_two, kernel_three, upstream
):
    frames, rows, cols, channels = layer_input.shape
    ta_n, ha_n = lax.axis_size("ta"), lax.axis_size("ha")
    scale = 1.0 / math.sqrt(frames * rows * cols * ta_n * ha_n)
    piece = channels // ha_n
    term_shape = (ha_n // 2, 2, 2, 2, 7, piece, channels)
    sems = reduce_sems(ha_n // 2)
    anywhere = pl.BlockSpec(memory_space=pl.ANY)
    half = jnp.bfloat16
    scratch = (
        [pltpu.VMEM(layer_input.shape, half)] * 3
        + [pltpu.VMEM(kernel_one.shape, half)] * 3
        + [pltpu.VMEM((frames + 2, rows + 2, cols, channels), half)] * 3
        + [pltpu.VMEM(term_shape, half)] * 3
        + [
            pltpu.VMEM((frames + 2, rows + 2, cols, 3 * channels), half),
            pltpu.VMEM((9, 3 * channels, channels), half),
            pltpu.VMEM((frames, channels, rows * cols), half),
            pltpu.VMEM((frames, rows * cols, channels), jnp.float32),
        ]
        + reduce_shapes(term_shape) * 3
        + [
            pltpu.SemaphoreType.DMA((6,)),
            pltpu.SemaphoreType.DMA((3, 5)),
            pltpu.SemaphoreType.DMA((3, 5)),
            pltpu.SemaphoreType.DMA((3, sems)),
            pltpu.SemaphoreType.DMA((3, sems)),
        ]
    )
    result = pl.pallas_call(
        functools.partial(whole_kernel, ta_n, ha_n, scale),
        out_shape=[jax.ShapeDtypeStruct(layer_input.shape, half)]
        + [jax.ShapeDtypeStruct((27, piece, channels), jnp.float32)] * 3,
        in_specs=[VMEM] * 2 + [anywhere] * 6,
        out_specs=[VMEM] * 4,
        scratch_shapes=scratch,
        compiler_params=pltpu.CompilerParams(
            collective_id=0, has_side_effects=True, vmem_limit_bytes=56 * 1024 * 1024
        ),
        name="backward",
    )(upstream, pre_three, pre_two, pre_one, layer_input, kernel_three, kernel_two, kernel_one)
    input_gradient, *sums = result
    three, two, one = [total.reshape(3, 3, 3, piece, channels) for total in sums]
    return (input_gradient, one, two, three)


def solution(mesh):
    return jax.shard_map(
        shards,
        mesh=mesh,
        in_specs=(
            P("ta", "ha", None, None),
            P("ta", "ha", None, None),
            P("ta", "ha", None, None),
            P("ta", "ha", None, None),
            P(),
            P(),
            P(),
            P("ta", "ha", None, None),
        ),
        out_specs=(
            P("ta", "ha", None, None),
            P(None, None, None, "ha", None),
            P(None, None, None, "ha", None),
            P(None, None, None, "ha", None),
        ),
        check_vma=False,
    )
```

time: 97.4 us -> 59.5 us (0.61)
  Pallas kernels: 81.2 us -> 54.1 us
  local copies, waits for them, and re-layouts: 12.9 us -> 4.46 us
  other arithmetic: 2.09 us -> 0 us
    pallas_call x7 -> x1, Pallas kernels: 81.2 us -> 54.1 us  [shards(): pl.pallas_call(functools.partial(whole_kernel, ta_n, ha_n, scale), out_sh...]
    transpose x3 -> x0, local copies, waits for them, and re-layouts: 4.7 us -> none  [shards(): flipped = jnp.swapaxes(kernel, 3, 4).reshape(9, 3 * channels, channels)]
    unnamed x29 -> x10, local copies, waits for them, and re-layouts: 8.23 us -> 4.46 us
    convert_element_type x1 -> x0, other arithmetic: 2.09 us -> none  [shards(): (upstream.astype(jnp.float32) * silu_slope(pre_three)).astype(jnp.bfloat16)]
where the time goes in v3:
time: 59.5 us; the launch traced here: 59.2 us
  Pallas kernels  54.1 us (91%)
  local copies, waits for them, and re-layouts  4.46 us (7%)
  between operations  0.65 us (1%)
    pallas_call x1, Pallas kernels, shards(): pl.pallas_call(functools.partial(whole_kernel, ta_n, ha_n, scale), out_sh...  54.1 us
    unnamed x10, local copies, waits for them, and re-layouts  4.46 us

profile of v3, /device:TPU:0, one launch (start us, length us, event | category | flops | bytes accessed | tf_op | source)
XLA Modules:
  0.0 59.2 jit_solution(10522844777661643629)
XLA Ops:
  0.6 54.1 %backward.1 = (bf16[2,3,192,128]{3,2,1,0:T(8,128)(2,1)}, f32[27,16,128]{2,1,0:T(8,128)}, f32[27,16,128]{2,1,0:T(8,128)}, f32[27,16,128]{2,1,0:T(8,128)}) custom-call(bf16[2,3,192,128]{3,2,1,0:T(8,128)(2,1)} %refs_0_.1, bf16[2,3,192,128]{3,2,1,0:T(8,128)(2,1)} %refs_1_.1, bf16[2,3,192,128]{3,2,1,0:T(8,128)(2,1)} %refs_2_.1, bf16[2,3,192,128]{3,2,1,0:T(8,128)(2,1)} %refs_3_.1, ...), custom_call_target="tpu_custom_call" | custom-call | tf_op jit(solution)/shard_map/backward/pallas_call | solution.py:409
  54.8 0.0 copy-start.2
  54.8 1.7 %copy.16 = bf16[2,3,192,128]{3,2,1,0:T(8,128)(2,1)} copy(bf16[2,3,192,128]{3,2,1,0:T(8,128)(2,1)} %get-tuple-element.16) | data formatting | bytes 589824
  56.5 0.0 copy-done.2
  56.5 0.0 copy-start.1
  56.5 0.7 %copy.17 = f32[3,3,3,16,128]{4,3,2,1,0:T(8,128)} copy(f32[3,3,3,16,128]{4,3,2,1,0:T(8,128)S(1)} %bitcast.5) | data formatting | bytes 442368
  57.2 0.3 copy-done.1
  57.5 0.0 copy-start
  57.5 0.7 %copy.18 = f32[3,3,3,16,128]{4,3,2,1,0:T(8,128)} copy(f32[3,3,3,16,128]{4,3,2,1,0:T(8,128)S(1)} %bitcast.4) | data formatting | bytes 442368
  58.2 0.3 copy-done
  58.6 0.7 %copy.19 = f32[3,3,3,16,128]{4,3,2,1,0:T(8,128)} copy(f32[3,3,3,16,128]{4,3,2,1,0:T(8,128)S(1)} %bitcast.3) | data formatting | bytes 442368
Async XLA Ops:
  54.8 1.7 %copy-start.2 = (f32[27,16,128]{2,1,0:T(8,128)S(1)}, f32[27,16,128]{2,1,0:T(8,128)}, u32[]{:S(2)}) copy-start(f32[27,16,128]{2,1,0:T(8,128)} %get-tuple-element.9) | copy-start | bytes 663556
  56.5 1.0 %copy-start.1 = (f32[27,16,128]{2,1,0:T(8,128)S(1)}, f32[27,16,128]{2,1,0:T(8,128)}, u32[]{:S(2)}) copy-start(f32[27,16,128]{2,1,0:T(8,128)} %get-tuple-element.10) | copy-start | bytes 663556
  57.5 1.0 %copy-start = (f32[27,16,128]{2,1,0:T(8,128)S(1)}, f32[27,16,128]{2,1,0:T(8,128)}, u32[]{:S(2)}) copy-start(f32[27,16,128]{2,1,0:T(8,128)} %get-tuple-element.11) | copy-start | bytes 663556

commit v4 on v3

--- a/solution.py
+++ b/solution.py
@@ -35,11 +35,14 @@
         )
 
     now, ahead = pl.ds(0, frames), pl.ds(frames, 2)
-    below = copy(0, wide.at[now, rows], wide.at[now, 0], 0, 1)
-    above = copy(1, wide.at[now, 1], wide.at[now, rows + 1], 0, -1)
-    earlier = copy(2, wide.at[now, pl.ds(1, rows)], wide.at[ahead, pl.ds(1, rows)], -1, 0)
-    corner_top = copy(3, wide.at[now, 0], wide.at[ahead, 0], -1, 0)
-    corner_end = copy(4, wide.at[now, rows + 1], wide.at[ahead, rows + 1], -1, 0)
+    each = range(frames)
+    below = [copy(1 + 4 * f, wide.at[f, rows], wide.at[f, 0], 0, 1) for f in each]
+    above = [copy(2 + 4 * f, wide.at[f, 1], wide.at[f, rows + 1], 0, -1) for f in each]
+    earlier = copy(0, wide.at[now, pl.ds(1, rows)], wide.at[ahead, pl.ds(1, rows)], -1, 0)
+    corner_top = [copy(3 + 4 * f, wide.at[f, 0], wide.at[frames + f, 0], -1, 0) for f in each]
+    corner_end = [
+        copy(4 + 4 * f, wide.at[f, rows + 1], wide.at[frames + f, rows + 1], -1, 0) for f in each
+    ]
 
     def clear():
         zero_row = jnp.zeros((frames,) + wide.shape[2:], wide.dtype)
@@ -60,39 +63,47 @@
                 wide[frames : frames + 2, row] = zero_row
 
     def start():
-        pl.when(has_down)(below.start)
-        pl.when(has_up)(above.start)
+        for f in each:
+            pl.when(has_down)(below[f].start)
+            pl.when(has_up)(above[f].start)
         pl.when(has_earlier)(earlier.start)
 
     def corners():
-        @pl.when(has_up)
-        def _():
-            below.wait_recv()
-            pl.when(has_earlier)(corner_top.start)
-
-        @pl.when(has_down)
-        def _():
-            above.wait_recv()
-            pl.when(has_earlier)(corner_end.start)
-
-    def arrive():
+        for f in each:
+
+            @pl.when(has_up)
+            def _():
+                below[f].wait_recv()
+                pl.when(has_earlier)(corner_top[f].start)
+
+            @pl.when(has_down)
+            def _():
+                above[f].wait_recv()
+                pl.when(has_earlier)(corner_end[f].start)
+
+    def arrive_block():
+        pl.when(has_later)(earlier.wait_recv)
+
+    def arrive_corners():
         @pl.when(has_later)
         def _():
-            earlier.wait_recv()
-            pl.when(has_up)(corner_top.wait_recv)
-            pl.when(has_down)(corner_end.wait_recv)
+            for f in each:
+                pl.when(has_up)(corner_top[f].wait_recv)
+                pl.when(has_down)(corner_end[f].wait_recv)
 
     def finish():
-        pl.when(has_down)(below.wait_send)
-        pl.when(has_up)(above.wait_send)
+        for f in each:
+            pl.when(has_down)(below[f].wait_send)
+            pl.when(has_up)(above[f].wait_send)
 
         @pl.when(has_earlier)
         def _():
             earlier.wait_send()
-            pl.when(has_up)(corner_top.wait_send)
-            pl.when(has_down)(corner_end.wait_send)
-
-    return clear, start, corners, arrive, finish
+            for f in each:
+                pl.when(has_up)(corner_top[f].wait_send)
+                pl.when(has_down)(corner_end[f].wait_send)
+
+    return clear, start, corners, arrive_block, arrive_corners, finish
 
 
 def shift(wide, shifted, f, first, count):
@@ -118,11 +129,13 @@
     return shifted[f + 2 - a, 2 - b : 2 - b + rows].reshape(rows * cols, width)
 
 
-def kernel_term(turned, shifted, term):
+def kernel_term(turned, shifted, term, steps=(0, 1, 2)):
     channels = turned.shape[1]
     pieces = term.shape[:2] + term.shape[5:]
     term[:, :, 1, 1, 6] = jnp.zeros(pieces, term.dtype)
     for a, b in TAPS:
+        if a not in steps:
+            continue
         total = None
         for f in range(turned.shape[0]):
             part = jnp.dot(turned[f], window(shifted, f, a, b), preferred_element_type=jnp.float32)
@@ -133,14 +146,20 @@
             term[:, :, tap // 14, tap // 7 % 2, tap % 7] = block.reshape(pieces)
 
 
-def back(shifted, flipped, f):
-    total = None
-    for a, b in TAPS:
-        part = jnp.dot(
-            window(shifted, f, a, b), flipped[a * 3 + b], preferred_element_type=jnp.float32
-        )
-        total = part if total is None else total + part
-    return total
+def back(shifted, flipped, sums, ahead, side):
+    frames = sums.shape[0]
+    for f in range(frames):
+        total = None
+        for a, b in TAPS:
+            if (f + 2 - a >= frames) != ahead or (b != 1) != side:
+                continue
+            part = jnp.dot(
+                window(shifted, f, a, b), flipped[a * 3 + b], preferred_element_type=jnp.float32
+            )
+            total = part if total is None else total + part
+        if ahead or side:
+            total = sums[f] + total
+        sums[f] = total
 
 
 def added(one, two):
@@ -220,6 +239,8 @@
         for row in range(half):
             cores[row] = added(term[row, :, :, core], from_core[row])
         low_x_copy.start()
+
+    def first_y():
         for row in range(half, depth):
             cores[row] = added(term[row, :, :, core], from_core[row])
         top_y_copy.start()
@@ -257,7 +278,7 @@
         for each in [core_copy, low_x_copy, low_y_copy, top_y_copy, top_x_copy] + z_copies + last_copies:
             each.wait_send()
 
-    return [start, first, second, third, fourth, finish]
+    return start, first, first_y, second, third, fourth, finish
 
 
 def greet(ha_n):
@@ -274,19 +295,20 @@
     def _():
         pl.semaphore_signal(barrier, inc=1, device_id=(other, ta), device_id_type=MESH)
 
-    pl.semaphore_wait(barrier, len(peers) + exists.astype(jnp.int32))
+    return lambda: pl.semaphore_wait(barrier, len(peers) + exists.astype(jnp.int32))
 
 
 def whole_kernel(ta_n, ha_n, scale, *refs):
     upstream, pre_three, saved_hbm, kernels_hbm = refs[0], refs[1], refs[2:5], refs[5:8]
     input_gradient, outs = refs[8], refs[9:12]
     saved, kernels, wides, terms = refs[12:15], refs[15:18], refs[18:21], refs[21:24]
-    shifted, flipped, turned, slopes = refs[24:28]
+    shifted, flipped, turned, slopes, totals = refs[24:29]
     load_sems, halo_send, halo_recv, send_sems, recv_sems = refs[-5:]
-    buffers = refs[28:-5]
+    buffers = refs[29:-5]
     each = len(buffers) // 3
     frames, rows, cols, channels = upstream.shape
     size = rows * cols
+    gathered = greet(ha_n)
 
     loads = [
         pltpu.make_async_copy(source, target, load_sems.at[n])
@@ -308,20 +330,24 @@
     for f in range(frames):
         values = upstream[f].astype(jnp.float32) * silu_slope(pre_three[f])
         wides[0][f, 1 : rows + 1] = values.astype(jnp.bfloat16)
-    greet(ha_n)
+    gathered()
     halos[0][1]()
-    for clear, _, _, _, _ in halos:
-        clear()
+    for each in halos:
+        each[0]()
 
     for n in range(3):
-        _, _, corners, arrive, _ = halos[n]
+        _, _, corners, arrive_block, arrive_corners, _ = halos[n]
         if n > 0:
             kernel_term(turned, shifted, terms[n - 1])
             sums[n - 1][0]()
-        if n > 1:
-            sums[n - 2][2]()
         loads[n].wait()
         loads[3 + n].wait()
+        for a, b in TAPS:
+            for c in range(3):
+                flipped[a * 3 + b, c * channels : (c + 1) * channels] = kernels[n][a, b, c].T
+        for f in range(frames):
+            shift(wides[n], shifted, f, 1, rows)
+        back(shifted, flipped, totals, False, False)
         for f in range(frames):
             values = saved[n][f].reshape(size, channels)
             if n < 2:
@@ -329,50 +355,49 @@
                 wide = values.astype(jnp.float32)
                 values = (wide * jax.nn.sigmoid(wide)).astype(jnp.bfloat16)
             turned[f] = values.T
-        for a, b in TAPS:
-            for c in range(3):
-                flipped[a * 3 + b, c * channels : (c + 1) * channels] = kernels[n][a, b, c].T
-        for f in range(frames):
-            shift(wides[n], shifted, f, 1, rows)
         corners()
+        if n > 0:
+            sums[n - 1][1]()
+        if n > 1:
+            sums[n - 2][3]()
         for f in range(frames):
             shift(wides[n], shifted, f, 0, 1)
             shift(wides[n], shifted, f, rows + 1, 1)
-        if n > 1:
-            sums[n - 2][3]()
-        arrive()
+        back(shifted, flipped, totals, False, True)
+        arrive_block()
+        for f in range(frames, frames + 2):
+            shift(wides[n], shifted, f, 1, rows)
+        back(shifted, flipped, totals, True, False)
+        if n == 2:
+            kernel_term(turned, shifted, terms[n], (2,))
+        arrive_corners()
         if n > 0:
-            sums[n - 1][1]()
+            sums[n - 1][2]()
         for f in range(frames, frames + 2):
-            shift(wides[n], shifted, f, 0, rows + 2)
+            shift(wides[n], shifted, f, 0, 1)
+            shift(wides[n], shifted, f, rows + 1, 1)
         if n == 2:
-            kernel_term(turned, shifted, terms[n])
+            kernel_term(turned, shifted, terms[n], (0, 1))
             sums[n][0]()
+            sums[n - 2][4]()
+        back(shifted, flipped, totals, True, True)
         for f in range(frames):
-            total = back(shifted, flipped, f)
             if n < 2:
-                total = total * slopes[f]
+                total = totals[f] * slopes[f]
                 wides[n + 1][f, 1 : rows + 1] = total.astype(jnp.bfloat16).reshape(
                     rows, cols, channels
                 )
             else:
-                input_gradient[f] = total.astype(jnp.bfloat16).reshape(rows, cols, channels)
-                if f == 0:
-                    sums[n][1]()
-                    sums[n - 1][2]()
+                total = totals[f].astype(jnp.bfloat16)
+                input_gradient[f] = total.reshape(rows, cols, channels)
         if n < 2:
             halos[n + 1][1]()
-    sums[0][4]()
-    sums[2][2]()
-    sums[1][3]()
-    sums[2][3]()
-    sums[1][4]()
-    sums[2][4]()
-    sums[0][5]()
-    sums[1][5]()
-    sums[2][5]()
+    for n, stage in (
+        (2, 1), (2, 2), (1, 3), (0, 5), (2, 3), (1, 4), (2, 4), (1, 5), (2, 5), (0, 6), (1, 6), (2, 6)
+    ):
+        sums[n][stage]()
     for halo in halos:
-        halo[4]()
+        halo[5]()
 
 
 def shards(
@@ -396,12 +421,13 @@
             pltpu.VMEM((9, 3 * channels, channels), half),
             pltpu.VMEM((frames, channels, rows * cols), half),
             pltpu.VMEM((frames, rows * cols, channels), jnp.float32),
+            pltpu.VMEM((frames, rows * cols, channels), jnp.float32),
         ]
         + reduce_shapes(term_shape) * 3
         + [
             pltpu.SemaphoreType.DMA((6,)),
-            pltpu.SemaphoreType.DMA((3, 5)),
-            pltpu.SemaphoreType.DMA((3, 5)),
+            pltpu.SemaphoreType.DMA((3, 1 + 4 * frames)),
+            pltpu.SemaphoreType.DMA((3, 1 + 4 * frames)),
             pltpu.SemaphoreType.DMA((3, sems)),
             pltpu.SemaphoreType.DMA((3, sems)),
         ]

time: 59.5 us -> 57.7 us (0.970)
  Pallas kernels: 54.1 us -> 52.3 us
    pallas_call x1, Pallas kernels: 54.1 us -> 52.3 us  [shards(): pl.pallas_call(functools.partial(whole_kernel, ta_n, ha_n, scale), out_sh...]
where the time goes in v4:
time: 57.7 us; the launch traced here: 57.5 us
  Pallas kernels  52.3 us (91%)
  local copies, waits for them, and re-layouts  4.46 us (8%)
  between operations  0.65 us (1%)
    pallas_call x1, Pallas kernels, shards(): pl.pallas_call(functools.partial(whole_kernel, ta_n, ha_n, scale), out_sh...  52.3 us
    unnamed x10, local copies, waits for them, and re-layouts  4.46 us

profile of v4, /device:TPU:0, one launch (start us, length us, event | category | flops | bytes accessed | tf_op | source)
XLA Modules:
  0.0 57.5 jit_solution(3120553933114638642)
XLA Ops:
  0.6 52.3 %backward.1 = (bf16[2,3,192,128]{3,2,1,0:T(8,128)(2,1)}, f32[27,16,128]{2,1,0:T(8,128)}, f32[27,16,128]{2,1,0:T(8,128)}, f32[27,16,128]{2,1,0:T(8,128)}) custom-call(bf16[2,3,192,128]{3,2,1,0:T(8,128)(2,1)} %refs_0_.1, bf16[2,3,192,128]{3,2,1,0:T(8,128)(2,1)} %refs_1_.1, bf16[2,3,192,128]{3,2,1,0:T(8,128)(2,1)} %refs_2_.1, bf16[2,3,192,128]{3,2,1,0:T(8,128)(2,1)} %refs_3_.1, ...), custom_call_target="tpu_custom_call" | custom-call | tf_op jit(solution)/shard_map/backward/pallas_call | solution.py:435
  53.0 0.0 copy-start.2
  53.0 1.7 %copy.16 = bf16[2,3,192,128]{3,2,1,0:T(8,128)(2,1)} copy(bf16[2,3,192,128]{3,2,1,0:T(8,128)(2,1)} %get-tuple-element.16) | data formatting | bytes 589824
  54.7 0.0 copy-done.2
  54.7 0.0 copy-start.1
  54.7 0.7 %copy.17 = f32[3,3,3,16,128]{4,3,2,1,0:T(8,128)} copy(f32[3,3,3,16,128]{4,3,2,1,0:T(8,128)S(1)} %bitcast.5) | data formatting | bytes 442368
  55.4 0.3 copy-done.1
  55.8 0.0 copy-start
  55.8 0.7 %copy.18 = f32[3,3,3,16,128]{4,3,2,1,0:T(8,128)} copy(f32[3,3,3,16,128]{4,3,2,1,0:T(8,128)S(1)} %bitcast.4) | data formatting | bytes 442368
  56.4 0.3 copy-done
  56.8 0.7 %copy.19 = f32[3,3,3,16,128]{4,3,2,1,0:T(8,128)} copy(f32[3,3,3,16,128]{4,3,2,1,0:T(8,128)S(1)} %bitcast.3) | data formatting | bytes 442368
Async XLA Ops:
  53.0 1.7 %copy-start.2 = (f32[27,16,128]{2,1,0:T(8,128)S(1)}, f32[27,16,128]{2,1,0:T(8,128)}, u32[]{:S(2)}) copy-start(f32[27,16,128]{2,1,0:T(8,128)} %get-tuple-element.9) | copy-start | bytes 663556
  54.7 1.0 %copy-start.1 = (f32[27,16,128]{2,1,0:T(8,128)S(1)}, f32[27,16,128]{2,1,0:T(8,128)}, u32[]{:S(2)}) copy-start(f32[27,16,128]{2,1,0:T(8,128)} %get-tuple-element.10) | copy-start | bytes 663556
  55.8 1.0 %copy-start = (f32[27,16,128]{2,1,0:T(8,128)S(1)}, f32[27,16,128]{2,1,0:T(8,128)}, u32[]{:S(2)}) copy-start(f32[27,16,128]{2,1,0:T(8,128)} %get-tuple-element.11) | copy-start | bytes 663556

commit v5 on v4

--- a/solution.py
+++ b/solution.py
@@ -400,6 +400,11 @@
         halo[5]()
 
 
+def settle(*refs):
+    for source, target in zip(refs[:4], refs[4:]):
+        target[...] = source[...]
+
+
 def shards(
     layer_input, pre_one, pre_two, pre_three, kernel_one, kernel_two, kernel_three, upstream
 ):
@@ -444,7 +449,13 @@
         ),
         name="backward",
     )(upstream, pre_three, pre_two, pre_one, layer_input, kernel_three, kernel_two, kernel_one)
-    input_gradient, *sums = result
+    input_gradient, *sums = pl.pallas_call(
+        settle,
+        out_shape=[jax.ShapeDtypeStruct(each.shape, each.dtype) for each in result],
+        in_specs=[VMEM] * 4,
+        out_specs=[VMEM] * 4,
+        name="settle",
+    )(*result)
     three, two, one = [total.reshape(3, 3, 3, piece, channels) for total in sums]
     return (input_gradient, one, two, three)
 

time: 57.7 us -> 55.3 us (0.958)
  local copies, waits for them, and re-layouts: 4.46 us -> 0 us
  Pallas kernels: 52.3 us -> 54.5 us
    unnamed x10 -> x0, local copies, waits for them, and re-layouts: 4.46 us -> none
    pallas_call x0 -> x1, Pallas kernels: none -> 2.19 us  [shards(): pl.pallas_call(settle, out_shape=[jax.ShapeDtypeStruct(each.shape, each.d...]
where the time goes in v5:
time: 55.3 us; the launch traced here: 55.1 us
  Pallas kernels  54.5 us (99%)
  between operations  0.64 us (1%)
    pallas_call x1, Pallas kernels, shards(): pl.pallas_call(functools.partial(whole_kernel, ta_n, ha_n, scale), out_sh...  52.3 us
    pallas_call x1, Pallas kernels, shards(): pl.pallas_call(settle, out_shape=[jax.ShapeDtypeStruct(each.shape, each.d...  2.19 us

profile of v5, /device:TPU:0, one launch (start us, length us, event | category | flops | bytes accessed | tf_op | source)
XLA Modules:
  0.0 55.1 jit_solution(4909966279410509754)
XLA Ops:
  0.6 52.3 %backward.1 = (bf16[2,3,192,128]{3,2,1,0:T(8,128)(2,1)}, f32[27,16,128]{2,1,0:T(8,128)}, f32[27,16,128]{2,1,0:T(8,128)}, f32[27,16,128]{2,1,0:T(8,128)}) custom-call(bf16[2,3,192,128]{3,2,1,0:T(8,128)(2,1)} %refs_0_.1, bf16[2,3,192,128]{3,2,1,0:T(8,128)(2,1)} %refs_1_.1, bf16[2,3,192,128]{3,2,1,0:T(8,128)(2,1)} %refs_2_.1, bf16[2,3,192,128]{3,2,1,0:T(8,128)(2,1)} %refs_3_.1, ...), custom_call_target="tpu_custom_call" | custom-call | tf_op jit(solution)/shard_map/backward/pallas_call | solution.py:440
  53.0 2.2 %settle.1 = (bf16[2,3,192,128]{3,2,1,0:T(8,128)(2,1)}, f32[27,16,128]{2,1,0:T(8,128)}, f32[27,16,128]{2,1,0:T(8,128)}, f32[27,16,128]{2,1,0:T(8,128)}) custom-call(bf16[2,3,192,128]{3,2,1,0:T(8,128)(2,1)} %get-tuple-element.12.refs_0_, f32[27,16,128]{2,1,0:T(8,128)} %get-tuple-element.13.refs_1_, f32[27,16,128]{2,1,0:T(8,128)} %get-tuple-element.14.refs_2_, ...), custom_call_target="tpu_custom_call" | custom-call | tf_op jit(solution)/shard_map/settle/pallas_call | solution.py:452
